TPU v7x, 256 devices: a whole 4x4x8 slice. The times are simulated.
256 devices in a mesh: seq: 32 (over z, x_hi, core), head: 8 (over y, x_lo).
Axes of the slice: x: 4 (x_hi: 2, x_lo: 2; x = x_hi * 2 + x_lo), y: 4, z: 8, core: 2. Of those that a mesh axis runs over, the one named last changes fastest.
Arguments:
- queries: bfloat16 [6144, 4096], P('seq', 'head'), may hold values from -64 to 64
- key_one: bfloat16 [6144, 128], P('seq'), may hold values from -6 to 6
- key_two: bfloat16 [6144, 128], P('seq'), may hold values from -6 to 6
- value_one: bfloat16 [6144, 128], P('seq'), may hold values from -6 to 6
- value_two: bfloat16 [6144, 128], P('seq'), may hold values from -6 to 6
- residual_in: bfloat16 [6144, 4096], P(('seq', 'head')), may hold values from -6 to 6
- out_weight: bfloat16 [4096, 4096], P('head'), may hold values from -0.5 to 0.5
- norm_gain: float32 [4096], replicated, may hold values from 0.1 to 1.9
- gate_weight: bfloat16 [4096, 7168], P('seq', 'head'), may hold values from -0.09375 to 0.09375
- up_weight: bfloat16 [4096, 7168], P('seq', 'head'), may hold values from -0.09375 to 0.09375
Outputs:
- residual_out: bfloat16 [6144, 4096], P(('seq', 'head'))
- hidden: bfloat16 [6144, 7168], P('seq', 'head')
All inputs are finite; a program needn't handle non-finite values.
Results may differ from a plain program's by a relative error of at most 0.02.
Values may be sent and summed in bfloat16 or wider, within the bound.
No kernel may reach another device: no remote copies, remote signals or barrier semaphores. Data moves between devices by JAX's collectives and lax.ppermute only.
A program may use at most 64 MiB of HBM per device.

v0:
```python
import math

import jax
import jax.numpy as jnp
from jax import lax
from jax.sharding import PartitionSpec as P

W1 = 512
W2 = 32


def from_behind(block, axis, distance):
    devices = range(lax.axis_size(axis))
    route = [(i - distance, i) for i in devices if i - distance in devices]
    return lax.ppermute(block, axis, route)


def in_blocks(array, dim, devices):
    shape = array.shape
    tiles = array.reshape(*shape[:dim], devices, shape[dim] // devices, *shape[dim + 1 :])
    return jnp.moveaxis(tiles, dim, 0)


def summed_on_arrival(array, axis, dim):
    tiles = in_blocks(array, dim, lax.axis_size(axis))
    arrived = lax.all_to_all(tiles, axis, split_axis=0, concat_axis=0, tiled=True)
    return arrived.astype(jnp.float32).sum(axis=0)


def sent_to_all(array, axis):
    devices = lax.axis_size(axis)
    return lax.all_to_all(
        jnp.broadcast_to(array[None], (devices, *array.shape)), axis, 0, 0, tiled=True
    )


def in_order(tiles, dim):
    shape = list(tiles.shape[1:])
    shape[dim] *= tiles.shape[0]
    return jnp.moveaxis(tiles, 0, dim).reshape(shape)


def gathered_copies(array, axis, dim):
    tiles = sent_to_all(array, axis)
    return in_order(tiles, dim)


def in_one_piece(arrays, axis, dim, along):
    ends, at = ([], 0)
    for a in arrays[:-1]:
        at += a.shape[along]
        ends.append(at)
    both = jnp.concatenate(arrays, axis=along)
    return tuple(jnp.split(lax.all_gather(both, axis, axis=dim, tiled=True), ends, axis=along))


def normalize(summed, norm_gain):
    mean_square = jnp.mean(summed * summed, axis=1, keepdims=True)
    scaled = summed * lax.rsqrt(mean_square + 1e-05) * norm_gain
    return scaled.astype(jnp.bfloat16)


def windows(part, row_count):
    span = part.shape[0] - row_count + 1
    return jnp.stack(
        [part[span - 1 - offset : span - 1 - offset + row_count] for offset in range(span)], axis=1
    )


def attend(queries, far_keys, far_values, near_keys, near_values, first_key, first_query):
    row_count = queries.shape[0]
    width = far_keys.shape[1]
    heads = queries.shape[1] // width
    reach = far_keys.shape[0] - row_count
    span = near_keys.shape[1]
    block_rows = math.gcd(row_count, 16)
    factor = 2.5 * width ** (-0.5)
    grouped = queries.reshape(row_count, heads, width)

    def one_block(begin):
        query_block = lax.dynamic_slice_in_dim(grouped, begin, block_rows, 0)
        near_key_block = lax.dynamic_slice_in_dim(near_keys, begin, block_rows, 0)
        near_value_block = lax.dynamic_slice_in_dim(near_values, begin, block_rows, 0)
        key_block = lax.dynamic_slice_in_dim(far_keys, begin, block_rows + reach, 0)
        value_block = lax.dynamic_slice_in_dim(far_values, begin, block_rows + reach, 0)
        paired = (
            query_block.astype(jnp.float32)[:, :, None, :]
            * near_key_block.astype(jnp.float32)[:, None, :, :]
        ).astype(jnp.bfloat16)
        logits = lax.dot_general(
            paired.reshape(-1, width),
            key_block,
            (((1,), (1,)), ((), ())),
            preferred_element_type=jnp.float32,
        )
        logits = logits.reshape(block_rows, heads, span, block_rows + reach) * factor
        local = jnp.arange(block_rows, dtype=jnp.int32)[:, None]
        column = jnp.arange(block_rows + reach, dtype=jnp.int32)[None, :]
        inside = (column >= local) & (column <= local + reach) & (column + begin + first_key >= 0)
        earlier_ok = local + begin + first_query - jnp.arange(span, dtype=jnp.int32)[None, :] >= 0
        valid = inside[:, None, None, :] & earlier_ok[:, None, :, None]
        masked = jnp.where(valid, logits, -jnp.inf)
        highest = jnp.max(masked, axis=(2, 3), keepdims=True)
        expo = jnp.exp(masked - highest)
        probs = (expo / jnp.sum(expo, axis=(2, 3), keepdims=True)).astype(jnp.bfloat16)
        mixed = jnp.dot(
            probs.reshape(-1, block_rows + reach), value_block, preferred_element_type=jnp.float32
        )
        mixed = mixed.reshape(block_rows, heads, span, width)
        combined = jnp.sum(mixed * near_value_block.astype(jnp.float32)[:, None, :, :], axis=2)
        return combined.astype(jnp.bfloat16)

    begins = jnp.arange(row_count // block_rows, dtype=jnp.int32) * block_rows
    outputs = lax.map(one_block, begins)
    return outputs.reshape(row_count, heads * width)


def body(
    queries,
    key_one,
    key_two,
    value_one,
    value_two,
    residual_in,
    out_weight,
    norm_gain,
    gate_weight,
    up_weight,
):
    row_count = queries.shape[0]
    width = key_one.shape[1]
    seq_rank = lax.axis_index("seq")
    reach = W1 - 1
    near_reach = W2 - 1
    shifts = -(-reach // row_count)
    stacked = jnp.concatenate([key_one, value_one, key_two, value_two], axis=1)
    earlier = []
    for step in range(shifts, 0, -1):
        earlier.append(from_behind(stacked, "seq", step))
    extended = jnp.concatenate(earlier + [stacked], axis=0)
    far_part = extended[extended.shape[0] - row_count - reach :, : 2 * width]
    near_part = extended[extended.shape[0] - row_count - near_reach :, 2 * width :]
    near_keys = windows(near_part[:, :width], row_count)
    near_values = windows(near_part[:, width:], row_count)
    first_query = seq_rank * row_count
    attended = attend(
        queries,
        far_part[:, :width],
        far_part[:, width:],
        near_keys,
        near_values,
        first_query - reach,
        first_query,
    )
    summed = residual_in.astype(jnp.float32) + summed_on_arrival(
        jnp.dot(attended, out_weight, preferred_element_type=jnp.float32).astype(jnp.bfloat16),
        "head",
        0,
    )
    residual_out = summed.astype(jnp.bfloat16)
    normed = gathered_copies(normalize(summed, norm_gain), "head", 0)
    pieces = in_one_piece((gate_weight, up_weight), "seq", 0, 1)
    gate_sum = jnp.dot(normed, pieces[0], preferred_element_type=jnp.float32)
    up_sum = jnp.dot(normed, pieces[1], preferred_element_type=jnp.float32)
    hidden = (jax.nn.silu(gate_sum) * up_sum).astype(jnp.bfloat16)
    return (residual_out, hidden)


def solution(mesh):
    return jax.shard_map(
        body,
        mesh=mesh,
        in_specs=(
            P("seq", "head"),
            P("seq", None),
            P("seq", None),
            P("seq", None),
            P("seq", None),
            P(("seq", "head"), None),
            P("head", None),
            P(),
            P("seq", "head"),
            P("seq", "head"),
        ),
        out_specs=(P(("seq", "head"), None), P("seq", "head")),
        check_vma=False,
    )
```

profile of v0, /device:TPU:100, one launch (start us, length us, event | category | flops | bytes accessed | tf_op | source)
XLA Modules:
  0.0 242.0 jit_solution(6541096646189040270)
XLA Ops:
  10.6 1.9 collective-permute-start
  12.5 5.0 %collective-permute-start.2 = (bf16[192,512]{1,0:T(8,128)(2,1)S(1)}, bf16[192,512]{1,0:T(8,128)(2,1)S(1)}, u32[]{:S(2)}, u32[]{:S(2)}) collective-permute-start(bf16[192,512]{1,0:T(8,128)(2,1)S(1)} %constant_dynamic-update-slice_fusion), channel_id=1, source_target_pairs={{0,16},{8,24},{16,32},{24,40},{32,48},{40,56},{48,64},{56,72},{64,... | collective-permute-start | bytes 589832 | tf_op jit(solution)/shard_map/ppermute | solution.py:15
  17.5 5.3 %collective-permute-start.1 = (bf16[192,512]{1,0:T(8,128)(2,1)S(1)}, bf16[192,512]{1,0:T(8,128)(2,1)S(1)}, u32[]{:S(2)}, u32[]{:S(2)}) collective-permute-start(bf16[192,512]{1,0:T(8,128)(2,1)S(1)} %constant_dynamic-update-slice_fusion), channel_id=1, source_target_pairs={{0,24},{8,32},{16,40},{24,48},{32,56},{40,64},{48,72},{56,80},{64,... | collective-permute-start | bytes 589832 | tf_op jit(solution)/shard_map/ppermute | solution.py:15
  22.8 1.9 pad_maximum_fusion
  46.1 125.6 %while.10 = (s32[]{:T(128)}, bf16[12,16,4,128]{3,2,1,0:T(4,128)(2,1)S(1)}, s32[12]{0:T(128)S(1)}, s32[]{:T(128)}, s32[]{:T(128)}, /*index=5*/bf16[192,4,128]{2,1...) while((s32[]{:T(128)}, ...), condition=%wide.region_4.5_spmd, body=%wide.region_0.4_spmd.sunk | while | flops 567036800 | bytes 17345268 | solution.py:114
  53.2 1.6 fusion.104
  54.8 1.7 fusion.105
  63.6 1.6 fusion.104
  65.3 1.7 fusion.105
  74.1 1.6 fusion.104
  75.8 1.7 fusion.105
  84.6 1.6 fusion.104
  86.2 1.7 fusion.105
  95.1 1.6 fusion.104
  96.7 1.7 fusion.105
  105.5 1.6 fusion.104
  107.2 1.7 fusion.105
  116.0 1.6 fusion.104
  117.6 1.7 fusion.105
  128.1 1.7 fusion.105
  136.9 1.6 fusion.104
  138.6 1.7 fusion.105
  149.0 1.7 fusion.105
  157.9 1.6 fusion.104
  159.5 1.7 fusion.105
  168.3 1.6 fusion.104
  170.0 1.7 fusion.105
  171.7 3.2 %convolution_convert_fusion = bf16[192,4096]{1,0:T(8,128)(2,1)S(1)} fusion(bf16[512,4096]{1,0:T(8,128)(2,1)} %param.18, bf16[24,8,4,128]{3,2,1,0:T(4,128)(2,1)S(1)} %bitcast.166), kind=kOutput, calls=%fused_computation.39 | convolution fusion | flops 806092800 | bytes 5963776 | tf_op jit(solution)/shard_map/dot_general | solution.py:156
  174.9 26.1 %all_to_all.10 = bf16[8,24,4096]{2,1,0:T(8,128)(2,1)S(1)} all-to-all(bf16[8,24,4096]{2,1,0:T(8,128)(2,1)S(1)} %bitcast.163), channel_id=1, replica_groups=mesh['seq'=32,'head'=8] {'head'}, dimensions={0} | all-to-all | bytes 3145728 | tf_op jit(solution)/shard_map/all_to_all | solution.py:26
  202.9 21.7 %all_to_all.11 = bf16[8,24,4096]{2,1,0:T(8,128)(2,1)S(1)} all-to-all(bf16[8,24,4096]{2,1,0:T(8,128)(2,1)S(1)} %broadcast_in_dim.18), channel_id=1, replica_groups=mesh['seq'=32,'head'=8] {'head'}, dimensions={0} | all-to-all | bytes 3145728 | tf_op jit(solution)/shard_map/all_to_all | solution.py:32
  224.6 4.9 %fusion.20 = f32[192,896]{1,0:T(8,128)S(1)} fusion(bf16[192,4096]{1,0:T(8,128)(2,1)S(1)} %bitcast.164, bf16[4096,1792]{1,0:T(8,128)(2,1)} %all-gather.2.cloned.1.call-done), kind=kOutput, calls=%fused_computation.37 | convolution fusion | flops 1409286144 | bytes 9601024 | tf_op jit(solution)/shard_map/dot_general | solution.py:163
  229.5 5.6 %fusion.25 = bf16[192,896]{1,0:T(8,128)(2,1)} fusion(bf16[192,4096]{1,0:T(8,128)(2,1)S(1)} %bitcast.165, bf16[4096,1792]{1,0:T(8,128)(2,1)} %all-gather.2.cloned.1.call-done, f32[192,896]{1,0:T(8,128)S(1)} %fusion.20), kind=kOutput, calls=%fused_computation.164 | convolution fusion | flops 1410318336 | bytes 9945088 | tf_op jit(solution)/shard_map/dot_general | solution.py:164
  (250 shorter events, 81.4 us)
Async XLA Ops:
  7.2 18.3 %copy-start.3 = (bf16[192,128]{1,0:T(8,128)(2,1)S(1)}, bf16[192,128]{1,0:T(8,128)(2,1)}, u32[]{:S(2)}) copy-start(bf16[192,128]{1,0:T(8,128)(2,1)} %param.14) | copy-start | bytes 147460
  7.2 17.6 %copy-start.2 = (bf16[192,128]{1,0:T(8,128)(2,1)S(1)}, bf16[192,128]{1,0:T(8,128)(2,1)}, u32[]{:S(2)}) copy-start(bf16[192,128]{1,0:T(8,128)(2,1)} %param.16) | copy-start | bytes 147460
  7.2 18.2 %copy-start.1 = (bf16[192,512]{1,0:T(8,128)(2,1)S(1)}, bf16[192,512]{1,0:T(8,128)(2,1)}, u32[]{:S(2)}) copy-start(bf16[192,512]{1,0:T(8,128)(2,1)} %param.12) | copy-start | bytes 589828
  7.2 217.4 %all-gather.2.cloned.1.call-start = ((), (), s32[]{:S(2)}) async-start(), calls=%async_computation.2 | async-start | bytes 15138816 | tf_op jit(solution)/shard_map/all_gather | solution.py:54
  10.6 14.9 %collective-permute-start = (bf16[192,512]{1,0:T(8,128)(2,1)S(1)}, bf16[192,512]{1,0:T(8,128)(2,1)S(1)}, u32[]{:S(2)}, u32[]{:S(2)}) collective-permute-start(bf16[192,512]{1,0:T(8,128)(2,1)S(1)} %constant_dynamic-update-slice_fusion), channel_id=1, source_target_pairs={{0,8},{8,16},{16,24},{24,32},{32,40},{40,48},{48,56},{56,64},{64,7... | collective-permute-start | bytes 589832 | tf_op jit(solution)/shard_map/ppermute | solution.py:15
  12.5 33.4 %collective-permute-start.2 = (bf16[192,512]{1,0:T(8,128)(2,1)S(1)}, bf16[192,512]{1,0:T(8,128)(2,1)S(1)}, u32[]{:S(2)}, u32[]{:S(2)}) collective-permute-start(bf16[192,512]{1,0:T(8,128)(2,1)S(1)} %constant_dynamic-update-slice_fusion), channel_id=1, source_target_pairs={{0,16},{8,24},{16,32},{24,40},{32,48},{40,56},{48,64},{56,72},{64,... | collective-permute-start | bytes 589832 | tf_op jit(solution)/shard_map/ppermute | solution.py:15
  17.5 28.4 %collective-permute-start.1 = (bf16[192,512]{1,0:T(8,128)(2,1)S(1)}, bf16[192,512]{1,0:T(8,128)(2,1)S(1)}, u32[]{:S(2)}, u32[]{:S(2)}) collective-permute-start(bf16[192,512]{1,0:T(8,128)(2,1)S(1)} %constant_dynamic-update-slice_fusion), channel_id=1, source_target_pairs={{0,24},{8,32},{16,40},{24,48},{32,56},{40,64},{48,72},{56,80},{64,... | collective-permute-start | bytes 589832 | tf_op jit(solution)/shard_map/ppermute | solution.py:15
  200.9 0.9 copy-start
  200.9 1.1 copy-start.4
Sparse Core Ops, SparseCore 0:
  24.8 124.3 all-gather.1
where the time goes:
time: 243 us; the launch traced here: 242 us
  other arithmetic  61.7 us (25%)
  blocking collectives  47.7 us (20%)
  matrix products  46.8 us (19%)
  loops' own time  34.6 us (14%)
  local copies, waits for them, and re-layouts  24.5 us (10%)
  between operations  14.3 us (6%)
  starting transfers between devices  12.3 us (5%)
    another operation x1, loops' own time, attend(): outputs = lax.map(one_block, begins)  34.6 us
    all_to_all x1, blocking collectives, summed_on_arrival(): lax.all_to_all(tiles, axis, split_axis=0, concat_axis=0, tiled=True)  26.1 us
    all_to_all x1, blocking collectives, sent_to_all(): lax.all_to_all(jnp.broadcast_to(array[None], (devices, *array.shape)), ax...  21.7 us
    dot_general x12, matrix products, one_block(): jnp.dot(probs.reshape(-1, block_rows + reach), value_block, preferred_ele...  20.1 us
    unnamed x59, other arithmetic  19.7 us
    reduce_sum x12, other arithmetic, one_block(): jnp.sum(expo, axis=(2, 3), keepdims=True)  19.2 us
    dot_general x12, matrix products, one_block(): lax.dot_general(paired.reshape(-1, width), key_block, (((1,), (1,)), ((),...  13 us
    dynamic_slice x12, local copies, waits for them, and re-layouts, one_block(): lax.dynamic_slice_in_dim(near_values, begin, block_rows, 0)  12.4 us
  transfers between devices with their start and end apart: 4, of which 0 were waited for; matrix products, arithmetic and copies ran while one was open for 49% of the time, Pallas kernels for 0%

commit v1 on v0

v1 whole, which is shorter than its diff:
```python
import functools
import math

import jax
import jax.numpy as jnp
import numpy as np
from jax import lax
from jax.experimental import pallas as pl
from jax.experimental.pallas import tpu as pltpu
from jax.sharding import Mesh
from jax.sharding import PartitionSpec as P

LIMIT = 2.0 ** 90

def attention_kernel(heads, rank_ref, q_ref, far3_ref, far2_ref, far1_ref, own_ref, o_ref,
                     kt_ref, vx_ref, k2_ref, v2_ref, m_ref, acc_ref):
    rows, width = q_ref.shape[0], kt_ref.shape[0]
    span = 32
    third = far3_ref.shape[0]
    reach = third + 2 * rows
    total = reach + rows
    padded = kt_ref.shape[1]
    tile = 256
    rank = rank_ref[0]
    scale = 2.5 * width ** (-0.5) * math.log2(math.e)

    missing = jnp.maximum(reach - rows * rank, 0)
    k2_missing = jnp.where(rank == 0, span, 0)
    parts = [(far3_ref, 0, third), (far2_ref, third, rows), (far1_ref, third + rows, rows), (own_ref, reach, rows)]
    zero_pad = jnp.zeros((padded - total, width), jnp.bfloat16)
    keys = jnp.concatenate([ref[:, :width] for ref, _, _ in parts] + [zero_pad], axis=0)
    values = jnp.concatenate([ref[:, width:2 * width] for ref, _, _ in parts] + [zero_pad], axis=0)
    first = jnp.where(rank == 0, own_ref[0:16, :width].astype(jnp.float32),
             jnp.where(rank == 1, far1_ref[0:16, :width].astype(jnp.float32), far2_ref[0:16, :width].astype(jnp.float32)))[0:1]
    pos = lax.broadcasted_iota(jnp.int32, (padded, width), 0)
    absent = pos < missing
    keys = jnp.where(absent, jnp.broadcast_to(first, keys.shape), keys.astype(jnp.float32))
    kt_ref[...] = keys.T.astype(jnp.bfloat16)
    vx_ref[:, :width] = jnp.where(absent, 0.0, values.astype(jnp.float32)).astype(jnp.bfloat16)
    vx_ref[:, width:] = jnp.where(absent, 0.0, 1.0).astype(jnp.bfloat16)

    own2k = own_ref[:, 2 * width:3 * width].astype(jnp.float32)
    own2v = own_ref[:, 3 * width:4 * width].astype(jnp.float32)
    near2k = far1_ref[rows - span:, 2 * width:3 * width].astype(jnp.float32)
    near2v = far1_ref[rows - span:, 3 * width:4 * width].astype(jnp.float32)
    start = rank == 0
    k2 = jnp.concatenate([jnp.where(start, jnp.broadcast_to(own2k[0:1], near2k.shape), near2k), own2k], axis=0)
    v2 = jnp.concatenate([jnp.where(start, 0.0, near2v), own2v], axis=0)
    there = jnp.concatenate([jnp.where(start, 0.0, jnp.ones_like(near2v)), jnp.ones_like(own2v)], axis=0)
    for shift in range(8):
        kept = span + rows - shift
        k2_ref[shift, shift:] = k2[:kept]
        v2_ref[shift, shift:, :width] = v2[:kept]
        v2_ref[shift, shift:, width:] = there[:kept]

    def window(ref, offset):
        return ref[offset % 8, pl.ds(pl.multiple_of(span - offset // 8 * 8, 8), rows), :]

    row = lax.broadcasted_iota(jnp.int32, (rows, tile), 0)
    col = lax.broadcasted_iota(jnp.int32, (rows, tile), 1)
    early = col > row
    dot = functools.partial(jnp.dot, preferred_element_type=jnp.float32)

    def logits(offset, h):
        k2 = window(k2_ref, offset).astype(jnp.bfloat16)
        pair = q_ref[:, h * width:(h + 1) * width] * k2
        s = [dot(pair, kt_ref[:, i * tile:(i + 1) * tile]) for i in range(3)]
        return jnp.where(early, s[0], s[2]), s[1]

    def highest(offset, h):
        ends, middle = logits(offset, h)
        return jnp.max(jnp.maximum(ends, middle), axis=1, keepdims=True)

    def run():
        acc_ref[...] = jnp.zeros_like(acc_ref)

        def step(offset, _):
            v2 = window(v2_ref, offset)
            for h in range(heads):
                m = m_ref[h]
                m2 = jnp.concatenate([m, m], axis=1)
                ends, middle = logits(offset, h)
                ends = jnp.exp2(ends * scale - m2)
                middle = jnp.exp2(middle * scale - m2).astype(jnp.bfloat16)
                p0 = jnp.where(early, ends, 0.0).astype(jnp.bfloat16)
                p2 = jnp.where(early, 0.0, ends).astype(jnp.bfloat16)
                r = dot(jnp.concatenate([p0, middle, p2], axis=1), vx_ref[...])
                acc_ref[h] += r * v2
            return 0

        lax.fori_loop(0, span, step, 0)

    for h in range(heads):
        m_ref[h] = jnp.broadcast_to(highest(0, h) * scale, (rows, width))
    run()
    worst = jnp.max(jnp.where(acc_ref[:, :, width:] < LIMIT, 0.0, 1.0))

    @pl.when(worst > 0.0)
    def _():
        def climb(offset, _):
            for h in range(heads):
                m_ref[h] = jnp.maximum(m_ref[h], jnp.broadcast_to(highest(offset, h) * scale, (rows, width)))
            return 0

        lax.fori_loop(1, span, climb, 0)
        run()

    for h in range(heads):
        a = acc_ref[h]
        o_ref[:, h * width:(h + 1) * width] = (a[:, :width] / a[:, width:]).astype(jnp.bfloat16)


def attend(queries, far3, far2, far1, own, rank, kernel=attention_kernel):
    rows, cols = queries.shape
    width = own.shape[1] // 4
    heads = cols // width
    vm = pl.BlockSpec(memory_space=pltpu.VMEM)
    return pl.pallas_call(
        functools.partial(kernel, heads),
        out_shape=jax.ShapeDtypeStruct((rows, cols), jnp.bfloat16),
        in_specs=[pl.BlockSpec(memory_space=pltpu.SMEM)] + [vm] * 5,
        out_specs=vm,
        scratch_shapes=[
            pltpu.VMEM((width, 768), jnp.bfloat16),
            pltpu.VMEM((768, 2 * width), jnp.bfloat16),
            pltpu.VMEM((8, rows + 32, width), jnp.float32),
            pltpu.VMEM((8, rows + 32, 2 * width), jnp.float32),
            pltpu.VMEM((heads, rows, width), jnp.float32),
            pltpu.VMEM((heads, rows, 2 * width), jnp.float32),
        ],
        compiler_params=pltpu.CompilerParams(vmem_limit_bytes=48 * 2**20),
        cost_estimate=pl.CostEstimate(flops=30_000_000_000, bytes_accessed=2_000_000, transcendentals=12_000_000),
        name="attention",
    )(rank, queries, far3, far2, far1, own)


SEQ = ("z", "xh", "core")
HEAD = ("y", "xl")


def swapped(block, axis):
    return lax.ppermute(block, axis, [(0, 1), (1, 0)])


def from_behind(block, distance):
    devices = range(lax.axis_size(SEQ))
    route = [(i - distance, i) for i in devices if i - distance in devices]
    return lax.ppermute(block, SEQ, route)


def gathered_weight(gate_weight, up_weight):
    both = jnp.stack([gate_weight, up_weight], axis=0)
    mine = lax.all_to_all(both, "core", 0, 0, tiled=True)
    mine = mine.reshape(2 * gate_weight.shape[0], gate_weight.shape[1])
    other = swapped(mine, "xh")
    low = lax.axis_index("xh") == 0
    pair = jnp.concatenate([jnp.where(low, mine, other), jnp.where(low, other, mine)], axis=0)
    return lax.all_gather(pair, "z", axis=0, tiled=True)


def summed_on_arrival(array):
    rows, cols = array.shape
    devices = lax.axis_size(HEAD)
    tiles = array.reshape(devices, rows // devices, cols)
    arrived = lax.all_to_all(tiles, HEAD, split_axis=0, concat_axis=0, tiled=True)
    return arrived.astype(jnp.float32).sum(axis=0)


def sent_to_all(array):
    rows, cols = array.shape
    devices = lax.axis_size(HEAD)
    tiles = lax.all_to_all(jnp.broadcast_to(array[None], (devices, rows, cols)), HEAD, 0, 0, tiled=True)
    return tiles.reshape(devices * rows, cols)


def normalize(summed, norm_gain):
    mean_square = jnp.mean(summed * summed, axis=1, keepdims=True)
    scaled = summed * lax.rsqrt(mean_square + 1e-05) * norm_gain
    return scaled.astype(jnp.bfloat16)


def body(queries, key_one, key_two, value_one, value_two, residual_in, out_weight, norm_gain, gate_weight, up_weight):
    weight = gathered_weight(gate_weight, up_weight)
    rank = lax.axis_index(SEQ).astype(jnp.int32).reshape(1)
    rows = queries.shape[0]
    far = jnp.concatenate([key_one, value_one], axis=1)
    own = jnp.concatenate([far, key_two, value_two], axis=1)
    far1 = from_behind(own, 1)
    far2 = from_behind(far, 2)
    far3 = from_behind(far[3 * rows - 512 :], 3)
    attended = attend(queries, far3, far2, far1, own, rank)
    partial = jnp.dot(attended, out_weight, preferred_element_type=jnp.float32).astype(jnp.bfloat16)
    summed = residual_in.astype(jnp.float32) + summed_on_arrival(partial)
    residual_out = summed.astype(jnp.bfloat16)
    normed = sent_to_all(normalize(summed, norm_gain))
    others = swapped(normed, "core")
    ours = jnp.dot(normed, weight, preferred_element_type=jnp.float32)
    theirs = jnp.dot(others, weight, preferred_element_type=jnp.float32).astype(jnp.bfloat16)
    back = swapped(theirs, "core").astype(jnp.float32)
    gates = lax.axis_index("core") == 0
    gate_sum = jnp.where(gates, ours, back)
    up_sum = jnp.where(gates, back, ours)
    hidden = (jax.nn.silu(gate_sum) * up_sum).astype(jnp.bfloat16)
    return (residual_out, hidden)


def solution(mesh):
    fine = Mesh(np.asarray(mesh.devices).reshape(8, 2, 2, 4, 2), SEQ + HEAD)
    return jax.shard_map(
        body,
        mesh=fine,
        in_specs=(
            P(SEQ, HEAD),
            P(SEQ, None),
            P(SEQ, None),
            P(SEQ, None),
            P(SEQ, None),
            P(SEQ + HEAD, None),
            P(HEAD, None),
            P(),
            P(SEQ, HEAD),
            P(SEQ, HEAD),
        ),
        out_specs=(P(SEQ + HEAD, None), P(SEQ, HEAD)),
        check_vma=False,
    )
```

time: 243 us -> 157 us (0.65)
  other arithmetic: 61.7 us -> 3.37 us
  Pallas kernels: 0 us -> 35.9 us
  matrix products: 46.8 us -> 11.6 us
  loops' own time: 34.6 us -> 0 us
  local copies, waits for them, and re-layouts: 24.5 us -> 0.59 us
  waiting for transfers between devices: 0.03 us -> 21.6 us
  blocking collectives: 47.7 us -> 56.1 us
    pallas_call x0 -> x1, Pallas kernels: none -> 35.9 us  [attend(): pl.pallas_call(functools.partial(kernel, heads), out_shape=jax.ShapeDtype...]
    another operation x1 -> x0, loops' own time: 34.6 us -> none  [attend(): outputs = lax.map(one_block, begins)]
    dot_general x26 -> x2, matrix products: 43.6 us -> 10.6 us  [the longest x1 5.72 us: body(): ours = jnp.dot(normed, weight, preferred_element_type=jnp.float32)]
    ppermute x3 -> x6, waiting for transfers between devices: 0.01 us -> 21.5 us  [the longest x3 18.5 us: swapped(): return lax.ppermute(block, axis, [(0, 1), (1, 0)])]
    unnamed x59 -> x0, other arithmetic: 19.7 us -> none
    dynamic_slice x24 -> x0, local copies, waits for them, and re-layouts: 19.4 us -> none  [the longest x12 12.4 us: one_block(): lax.dynamic_slice_in_dim(near_values, begin, block_rows, 0)]
    reduce_sum x12 -> x0, other arithmetic: 19.2 us -> none  [one_block(): jnp.sum(expo, axis=(2, 3), keepdims=True)]
    all_to_all x2 -> x3, blocking collectives: 47.7 us -> 56.1 us  [the longest x1 28.1 us: summed_on_arrival(): lax.all_to_all(tiles, HEAD, split_axis=0, concat_axis=0, tiled=True)]
  transfers between devices with their start and end apart: 4 -> 7, of which waited for: 0 -> 4; matrix products, arithmetic and copies ran while one was open for 49% -> 1% of each run, Pallas kernels for 0% -> 23%
where the time goes in v1:
time: 157 us; the launch traced here: 156 us
  blocking collectives  56.1 us (36%)
  Pallas kernels  35.9 us (23%)
  waiting for transfers between devices  21.6 us (14%)
  between operations  14.3 us (9%)
  starting transfers between devices  13 us (8%)
  matrix products  11.6 us (7%)
  other arithmetic  3.37 us (2%)
    pallas_call x1, Pallas kernels, attend(): pl.pallas_call(functools.partial(kernel, heads), out_shape=jax.ShapeDtype...  35.9 us
    all_to_all x1, blocking collectives, summed_on_arrival(): lax.all_to_all(tiles, HEAD, split_axis=0, concat_axis=0, tiled=True)  28.1 us
    all_to_all x1, blocking collectives, sent_to_all(): lax.all_to_all(jnp.broadcast_to(array[None], (devices, rows, cols)), HEAD...  23.9 us
    ppermute x3, waiting for transfers between devices, swapped(): return lax.ppermute(block, axis, [(0, 1), (1, 0)])  18.5 us
    ppermute x3, starting transfers between devices, from_behind(): return lax.ppermute(block, SEQ, route)  12.2 us
    dot_general x1, matrix products, body(): ours = jnp.dot(normed, weight, preferred_element_type=jnp.float32)  5.72 us
    dot_general x1, matrix products, body(): jnp.dot(others, weight, preferred_element_type=jnp.float32)  4.89 us
    all_to_all x1, blocking collectives, gathered_weight(): mine = lax.all_to_all(both, 'core', 0, 0, tiled=True)  4.1 us
  transfers between devices with their start and end apart: 7, of which 4 were waited for; matrix products, arithmetic and copies ran while one was open for 1% of the time, Pallas kernels for 23%

profile of v1, /device:TPU:100, one launch (start us, length us, event | category | flops | bytes accessed | tf_op | source)
XLA Modules:
  0.0 156.4 jit_solution(5540282664348400927)
XLA Ops:
  7.2 0.0 all-gather.2.cloned.1.call-start
  7.2 1.1 pad_maximum_fusion.1
  8.3 4.1 %all_to_all.15 = bf16[2,128,896]{2,1,0:T(8,128)(2,1)S(1)} all-to-all(bf16[2,128,896]{2,1,0:T(8,128)(2,1)S(1)} %pad_maximum_fusion.1), channel_id=1, replica_groups=mesh['z'=8,'xh'=2,'core'=2,'y'=4,'xl'=2] {'core'}, dimensions={0} | all-to-all | bytes 917504 | tf_op jit(solution)/shard_map/all_to_all | solution.py:153
  12.4 0.5 collective-permute-start.3
  12.9 13.6 %collective-permute-done.3 = bf16[256,896]{1,0:T(8,128)(2,1)S(1)} collective-permute-done((bf16[256,896]{1,0:T(8,128)(2,1)S(1)}, bf16[256,896]{1,0:T(8,128)(2,1)S(1)}, u32[]{:S(2)}, u32[]{:S(2)}) %collective-permute-start.3) | collective-permute-done | bytes 458784 | tf_op jit(solution)/shard_map/ppermute | solution.py:142
  26.5 0.1 broadcast_select_fusion.1
  26.6 0.0 copy-start.5
  26.6 0.0 copy-start.6
  26.6 0.0 copy-start.3
  26.6 0.0 copy-start.4
  26.7 0.0 copy-start
  26.7 1.0 pad_maximum_fusion
  27.7 0.0 all-gather.2.cloned.1.call-update
  27.9 1.9 %collective-permute-start.2 = (bf16[192,512]{1,0:T(8,128)(2,1)S(1)}, bf16[192,512]{1,0:T(8,128)(2,1)S(1)}, u32[]{:S(2)}, u32[]{:S(2)}) collective-permute-start(bf16[192,512]{1,0:T(8,128)(2,1)S(1)} %constant_dynamic-update-slice_fusion.2.own_ref), channel_id=1, source_target_pairs={{0,8},{8,16},{16,24},{24,32},{32,40},{40,48},{48,56},{56,64},{64,7... | collective-permute-start | bytes 589832 | tf_op jit(solution)/shard_map/ppermute | solution.py:148
  29.8 5.0 %collective-permute-start.1 = (bf16[192,256]{1,0:T(8,128)(2,1)S(1)}, bf16[192,256]{1,0:T(8,128)(2,1)S(1)}, u32[]{:S(2)}, u32[]{:S(2)}) collective-permute-start(bf16[192,256]{1,0:T(8,128)(2,1)S(1)} %get-tuple-element.7), channel_id=1, source_target_pairs={{0,16},{8,24},{16,32},{24,40},{32,48},{40,56},{48,64},{56,72},{64,... | collective-permute-start | bytes 294920 | tf_op jit(solution)/shard_map/ppermute | solution.py:148
  34.8 5.3 %collective-permute-start = (bf16[128,256]{1,0:T(8,128)(2,1)S(1)}, bf16[128,256]{1,0:T(8,128)(2,1)S(1)}, u32[]{:S(2)}, u32[]{:S(2)}) collective-permute-start(bf16[128,256]{1,0:T(8,128)(2,1)S(1)} %slice.4), channel_id=1, source_target_pairs={{0,24},{8,32},{16,40},{24,48},{32,56},{40,64},{48,72},{56,80},{64,... | collective-permute-start | bytes 196616 | tf_op jit(solution)/shard_map/ppermute | solution.py:148
  40.1 3.1 %collective-permute-done.far3_ref = bf16[128,256]{1,0:T(8,128)(2,1)S(1)} collective-permute-done((bf16[128,256]{1,0:T(8,128)(2,1)S(1)}, bf16[128,256]{1,0:T(8,128)(2,1)S(1)}, u32[]{:S(2)}, u32[]{:S(2)}) %collective-permute-start) | collective-permute-done | bytes 65568 | tf_op jit(solution)/shard_map/ppermute | solution.py:148
  43.2 35.9 %attention.1 = bf16[192,512]{1,0:T(8,128)(2,1)S(1)} custom-call(s32[1]{0:T(128)} %bitcast.rank_ref, bf16[192,512]{1,0:T(8,128)(2,1)S(1)} %copy-done, bf16[128,256]{1,0:T(8,128)(2,1)S(1)} %collective-permute-done.far3_ref, bf16[192,256]{1,0:T(8,128)(2,1)S(1)} %collective-permute-done.1.far2_ref, bf16[192,512]{1,0:T(8,128)(2,1)S(1)} %collective-permute-done.2.far1_ref, ...), custom_call_target="tpu_custom_call" | custom-call | flops 30000001024 | bytes 2000000 | tf_op jit(solution)/shard_map/attention/pallas_call | solution.py:118
  79.2 1.0 convolution_convert_fusion
  80.2 0.0 copy-start.2
  80.2 28.1 %all_to_all.16 = bf16[8,24,4096]{2,1,0:T(8,128)(2,1)S(1)} all-to-all(bf16[8,24,4096]{2,1,0:T(8,128)(2,1)S(1)} %bitcast.14), channel_id=1, replica_groups=mesh['z'=8,'xh'=2,'core'=2,'y'=4,'xl'=2] {'y','xl'}, dimensions={0} | all-to-all | bytes 3145728 | tf_op jit(solution)/shard_map/all_to_all | solution.py:165
  108.3 0.2 convert_reduce_fusion
  108.5 0.2 multiply_reduce_fusion
  108.7 0.3 copy-done.7
  109.0 0.7 multiply_convert_fusion
  109.7 0.2 broadcast_in_dim.2
  109.9 23.9 %all_to_all.17 = bf16[8,24,4096]{2,1,0:T(8,128)(2,1)S(1)} all-to-all(bf16[8,24,4096]{2,1,0:T(8,128)(2,1)S(1)} %broadcast_in_dim.2), channel_id=1, replica_groups=mesh['z'=8,'xh'=2,'core'=2,'y'=4,'xl'=2] {'y','xl'}, dimensions={0} | all-to-all | bytes 3145728 | tf_op jit(solution)/shard_map/all_to_all | solution.py:172
  133.8 3.4 %collective-permute-done.4 = bf16[192,4096]{1,0:T(8,128)(2,1)S(1)} collective-permute-done((bf16[192,4096]{1,0:T(8,128)(2,1)S(1)}, bf16[192,4096]{1,0:T(8,128)(2,1)S(1)}, u32[]{:S(2)}, u32[]{:S(2)}) %collective-permute-start.4) | collective-permute-done | bytes 1572896 | tf_op jit(solution)/shard_map/ppermute | solution.py:142
  137.2 4.9 %convolution_convert_fusion.1 = bf16[192,896]{1,0:T(8,128)(2,1)S(1)} fusion(bf16[192,4096]{1,0:T(8,128)(2,1)S(1)} %collective-permute-done.4, bf16[4096,896]{1,0:T(8,128)(2,1)} %all-gather.2.cloned.1.call-done), kind=kOutput, calls=%fused_computation.2 | convolution fusion | flops 1409458176 | bytes 9256960 | tf_op jit(solution)/shard_map/dot_general | solution.py:198
  142.1 0.2 collective-permute-start.5
  142.3 1.5 collective-permute-done.5
  143.8 5.7 %fusion.1 = bf16[192,896]{1,0:T(8,128)(2,1)} fusion(bf16[192,896]{1,0:T(8,128)(2,1)S(1)} %collective-permute-done.5, pred[]{:T(512)S(6)} %eq.6, bf16[192,4096]{1,0:T(8,128)(2,1)S(1)} %bitcast.17, bf16[4096,896]{1,0:T(8,128)(2,1)} %all-gather.2.cloned.1.call-done), kind=kOutput, calls=%fused_computation.7 | convolution fusion | flops 1410834432 | bytes 9601025 | tf_op jit(solution)/shard_map/dot_general | solution.py:197
  (19 shorter events, 0.1 us)
Async XLA Ops:
  7.2 130.0 %all-gather.2.cloned.1.call-start = ((), (), s32[]{:S(2)}) async-start(), calls=%async_computation.3 | async-start | bytes 8257536 | tf_op jit(solution)/shard_map/all_gather | solution.py:158
  12.4 14.1 %collective-permute-start.3 = (bf16[256,896]{1,0:T(8,128)(2,1)S(1)}, bf16[256,896]{1,0:T(8,128)(2,1)S(1)}, u32[]{:S(2)}, u32[]{:S(2)}) collective-permute-start(bf16[256,896]{1,0:T(8,128)(2,1)S(1)} %bitcast.15), channel_id=1, source_target_pairs={{0,16},{16,0},{1,17},{17,1},{2,18},{18,2},{3,19},{19,3},{4,20},{20... | collective-permute-start | bytes 1376264 | tf_op jit(solution)/shard_map/ppermute | solution.py:142
  26.6 1.1 copy-start.5
  26.6 1.1 copy-start.6
  26.6 1.2 copy-start.3
  26.6 1.2 copy-start.4
  26.7 16.6 %copy-start = (bf16[192,512]{1,0:T(8,128)(2,1)S(1)}, bf16[192,512]{1,0:T(8,128)(2,1)}, u32[]{:S(2)}) copy-start(bf16[192,512]{1,0:T(8,128)(2,1)} %q_ref.1) | copy-start | bytes 589828
  27.9 15.3 %collective-permute-start.2 = (bf16[192,512]{1,0:T(8,128)(2,1)S(1)}, bf16[192,512]{1,0:T(8,128)(2,1)S(1)}, u32[]{:S(2)}, u32[]{:S(2)}) collective-permute-start(bf16[192,512]{1,0:T(8,128)(2,1)S(1)} %constant_dynamic-update-slice_fusion.2.own_ref), channel_id=1, source_target_pairs={{0,8},{8,16},{16,24},{24,32},{32,40},{40,48},{48,56},{56,64},{64,7... | collective-permute-start | bytes 589832 | tf_op jit(solution)/shard_map/ppermute | solution.py:148
  29.8 13.4 %collective-permute-start.1 = (bf16[192,256]{1,0:T(8,128)(2,1)S(1)}, bf16[192,256]{1,0:T(8,128)(2,1)S(1)}, u32[]{:S(2)}, u32[]{:S(2)}) collective-permute-start(bf16[192,256]{1,0:T(8,128)(2,1)S(1)} %get-tuple-element.7), channel_id=1, source_target_pairs={{0,16},{8,24},{16,32},{24,40},{32,48},{40,56},{48,64},{56,72},{64,... | collective-permute-start | bytes 294920 | tf_op jit(solution)/shard_map/ppermute | solution.py:148
  34.8 8.4 %collective-permute-start = (bf16[128,256]{1,0:T(8,128)(2,1)S(1)}, bf16[128,256]{1,0:T(8,128)(2,1)S(1)}, u32[]{:S(2)}, u32[]{:S(2)}) collective-permute-start(bf16[128,256]{1,0:T(8,128)(2,1)S(1)} %slice.4), channel_id=1, source_target_pairs={{0,24},{8,32},{16,40},{24,48},{32,56},{40,64},{48,72},{56,80},{64,... | collective-permute-start | bytes 196616 | tf_op jit(solution)/shard_map/ppermute | solution.py:148
  43.2 35.9 %copy-start.1 = (bf16[512,4096]{1,0:T(8,128)(2,1)S(1)}, bf16[512,4096]{1,0:T(8,128)(2,1)}, u32[]{:S(2)}) copy-start(bf16[512,4096]{1,0:T(8,128)(2,1)} %param.16) | copy-start | bytes 12582916
  80.2 28.4 %copy-start.2 = (bf16[24,4096]{1,0:T(8,128)(2,1)S(1)}, bf16[24,4096]{1,0:T(8,128)(2,1)}, u32[]{:S(2)}) copy-start(bf16[24,4096]{1,0:T(8,128)(2,1)} %param.15) | copy-start | bytes 589828
  108.3 0.7 copy-start.7
  133.8 3.4 %collective-permute-start.4 = (bf16[192,4096]{1,0:T(8,128)(2,1)S(1)}, bf16[192,4096]{1,0:T(8,128)(2,1)S(1)}, u32[]{:S(2)}, u32[]{:S(2)}) collective-permute-start(bf16[192,4096]{1,0:T(8,128)(2,1)S(1)} %bitcast.16), channel_id=1, source_target_pairs={{0,8},{8,0},{1,9},{9,1},{2,10},{10,2},{3,11},{11,3},{4,12},{12,4},... | collective-permute-start | bytes 4718600 | tf_op jit(solution)/shard_map/ppermute | solution.py:142
  142.1 1.7 %collective-permute-start.5 = (bf16[192,896]{1,0:T(8,128)(2,1)S(1)}, bf16[192,896]{1,0:T(8,128)(2,1)S(1)}, u32[]{:S(2)}, u32[]{:S(2)}) collective-permute-start(bf16[192,896]{1,0:T(8,128)(2,1)S(1)} %convolution_convert_fusion.1), channel_id=1, source_target_pairs={{0,8},{8,0},{1,9},{9,1},{2,10},{10,2},{3,11},{11,3},{4,12},{12,4},... | collective-permute-start | bytes 1032200 | tf_op jit(solution)/shard_map/ppermute | solution.py:142
Sparse Core Ops, SparseCore 0:
  27.8 85.4 all-gather.1

commit v2 on v1

v2 whole, which is shorter than its diff:
```python
import functools
import math

import jax
import jax.numpy as jnp
import numpy as np
from jax import lax
from jax.experimental import pallas as pl
from jax.experimental.pallas import tpu as pltpu
from jax.sharding import Mesh
from jax.sharding import PartitionSpec as P

LIMIT = 2.0 ** 90


def attention_kernel(heads, begin, stack, rank_ref, q_ref, far3_ref, far2_ref, far1_ref, own_ref, o_ref,
                     kt_ref, vx_ref, k2_ref, v2_ref, m_ref, acc_ref):
    count, width = q_ref.shape[0], kt_ref.shape[0]
    rows = own_ref.shape[0]
    groups = 8
    size, apart = count // groups, rows // groups
    span = 32
    third = far3_ref.shape[0]
    reach = third + 2 * rows
    total = reach + rows
    padded = kt_ref.shape[1]
    tile = 256
    rank = rank_ref[0]
    scale = 2.5 * width ** (-0.5) * math.log2(math.e)

    missing = jnp.maximum(reach - rows * rank, 0)
    k2_missing = jnp.where(rank == 0, span, 0)
    parts = [(far3_ref, 0, third), (far2_ref, third, rows), (far1_ref, third + rows, rows), (own_ref, reach, rows)]
    zero_pad = jnp.zeros((padded - total, width), jnp.bfloat16)
    keys = jnp.concatenate([ref[:, :width] for ref, _, _ in parts] + [zero_pad], axis=0)
    values = jnp.concatenate([ref[:, width:2 * width] for ref, _, _ in parts] + [zero_pad], axis=0)
    first = jnp.where(rank == 0, own_ref[0:16, :width].astype(jnp.float32),
             jnp.where(rank == 1, far1_ref[0:16, :width].astype(jnp.float32), far2_ref[0:16, :width].astype(jnp.float32)))[0:1]
    pos = lax.broadcasted_iota(jnp.int32, (padded, width), 0)
    absent = pos < missing
    keys = jnp.where(absent, jnp.broadcast_to(first, keys.shape), keys.astype(jnp.float32))
    kt_ref[...] = keys.T.astype(jnp.bfloat16)
    vx_ref[:, :width] = jnp.where(absent, 0.0, values.astype(jnp.float32)).astype(jnp.bfloat16)
    vx_ref[:, width:] = jnp.where(absent, 0.0, 1.0).astype(jnp.bfloat16)

    own2k = own_ref[:, 2 * width:3 * width].astype(jnp.float32)
    own2v = own_ref[:, 3 * width:4 * width].astype(jnp.float32)
    near2k = far1_ref[rows - span:, 2 * width:3 * width].astype(jnp.float32)
    near2v = far1_ref[rows - span:, 3 * width:4 * width].astype(jnp.float32)
    start = rank == 0
    k2 = jnp.concatenate([jnp.where(start, jnp.broadcast_to(own2k[0:1], near2k.shape), near2k), own2k], axis=0)
    v2 = jnp.concatenate([jnp.where(start, 0.0, near2v), own2v], axis=0)
    there = jnp.concatenate([jnp.where(start, 0.0, jnp.ones_like(near2v)), jnp.ones_like(own2v)], axis=0)
    for shift in range(8):
        kept = span + rows - shift
        k2_ref[shift, shift:] = k2[:kept]
        v2_ref[shift, shift:, :width] = v2[:kept]
        v2_ref[shift, shift:, width:] = there[:kept]

    def window(ref, offset):
        base = span + begin - offset // 8 * 8
        return jnp.concatenate([ref[offset % 8, pl.ds(pl.multiple_of(base + apart * g, 8), size), :] for g in range(groups)], axis=0)

    def at(shape):
        index = lax.broadcasted_iota(jnp.int32, shape, 0) % count
        return index // size * apart + index % size + begin

    def is_early(copies):
        shape = (copies * heads * count, tile)
        return lax.broadcasted_iota(jnp.int32, shape, 1) > at(shape)

    dot = functools.partial(jnp.dot, preferred_element_type=jnp.float32)

    def logits(offsets):
        pairs = []
        for offset in offsets:
            k2 = window(k2_ref, offset).astype(jnp.bfloat16)
            pairs += [q_ref[:, h * width:(h + 1) * width] * k2 for h in range(heads)]
        pair = jnp.concatenate(pairs, axis=0)
        return [dot(pair, kt_ref[:, i * tile:(i + 1) * tile]) for i in range(3)]

    def highest(offset):
        first, middle, last = logits([offset])
        return jnp.max(jnp.maximum(jnp.where(is_early(1), first, last), middle), axis=1, keepdims=True)

    def run():
        acc_ref[...] = jnp.zeros_like(acc_ref)

        def step(index, _):
            offsets = [index * stack + i for i in range(stack)]
            early = is_early(stack)
            first, middle, last = logits(offsets)
            m2 = jnp.concatenate([jnp.concatenate([m_ref[...]] * 2, axis=1)] * stack, axis=0)
            ends = jnp.exp2(jnp.where(early, first, last) * scale - m2)
            middle = jnp.exp2(middle * scale - m2).astype(jnp.bfloat16)
            p0 = jnp.where(early, ends, 0.0).astype(jnp.bfloat16)
            p2 = jnp.where(early, 0.0, ends).astype(jnp.bfloat16)
            r = dot(jnp.concatenate([p0, middle, p2], axis=1), vx_ref[...])
            for i, offset in enumerate(offsets):
                v2 = window(v2_ref, offset)
                for h in range(heads):
                    begins = (i * heads + h) * count
                    acc_ref[h * count:(h + 1) * count] += r[begins:begins + count] * v2
            return 0

        lax.fori_loop(0, span // stack, step, 0)

    m_ref[...] = jnp.broadcast_to(highest(0) * scale, m_ref.shape)
    run()
    worst = jnp.max(jnp.where(acc_ref[:, width:] < LIMIT, 0.0, 1.0))

    @pl.when(worst > 0.0)
    def _():
        def climb(offset, _):
            m_ref[...] = jnp.maximum(m_ref[...], jnp.broadcast_to(highest(offset) * scale, m_ref.shape))
            return 0

        lax.fori_loop(1, span, climb, 0)
        run()

    for h in range(heads):
        a = acc_ref[h * count:(h + 1) * count]
        o_ref[:, h * width:(h + 1) * width] = (a[:, :width] / a[:, width:]).astype(jnp.bfloat16)


def attend(queries, far3, far2, far1, own, rank, begin, stack):
    count, cols = queries.shape
    rows, width = own.shape[0], own.shape[1] // 4
    heads = cols // width
    vm = pl.BlockSpec(memory_space=pltpu.VMEM)
    return pl.pallas_call(
        functools.partial(attention_kernel, heads, begin, stack),
        out_shape=jax.ShapeDtypeStruct((count, cols), jnp.bfloat16),
        in_specs=[pl.BlockSpec(memory_space=pltpu.SMEM)] + [vm] * 5,
        out_specs=vm,
        scratch_shapes=[
            pltpu.VMEM((width, 768), jnp.bfloat16),
            pltpu.VMEM((768, 2 * width), jnp.bfloat16),
            pltpu.VMEM((8, rows + 32, width), jnp.float32),
            pltpu.VMEM((8, rows + 32, 2 * width), jnp.float32),
            pltpu.VMEM((heads * count, width), jnp.float32),
            pltpu.VMEM((heads * count, 2 * width), jnp.float32),
        ],
        compiler_params=pltpu.CompilerParams(vmem_limit_bytes=48 * 2**20),
        cost_estimate=pl.CostEstimate(
            flops=count * heads * 32 * 1536 * 512, bytes_accessed=2_000_000, transcendentals=count * heads * 32 * 512
        ),
        name="attention",
    )(rank, queries, far3, far2, far1, own)


SEQ = ("z", "xh", "core")
HEAD = ("y", "xl")
PARTS = ((16, 8, 2), (0, 16, 1))
EARLY = 256


def swapped(block, axis):
    return lax.ppermute(block, axis, [(0, 1), (1, 0)])


def in_turn(axis, mine, other, dim):
    first = lax.axis_index(axis) == 0
    return jnp.concatenate([jnp.where(first, mine, other), jnp.where(first, other, mine)], axis=dim)


def from_behind(block, distance):
    devices = range(lax.axis_size(SEQ))
    route = [(i - distance, i) for i in devices if i - distance in devices]
    return lax.ppermute(block, SEQ, route)


def over_heads(tiles):
    return lax.all_to_all(tiles, HEAD, 0, 0, tiled=True)


def normalize(summed, norm_gain):
    mean_square = jnp.mean(summed * summed, axis=1, keepdims=True)
    scaled = summed * lax.rsqrt(mean_square + 1e-05) * norm_gain
    return scaled.astype(jnp.bfloat16)


def body(queries, key_one, key_two, value_one, value_two, residual_in, out_weight, norm_gain, gate_weight, up_weight):
    rows, cols = queries.shape
    peers = lax.axis_size(HEAD)
    apart = rows // peers
    planes = lax.axis_size("z")
    gates = lax.axis_index("core") == 0
    kept = jnp.where(gates, gate_weight, up_weight)
    sent = jnp.where(gates, up_weight, gate_weight)
    far = jnp.concatenate([key_one, value_one], axis=1)
    own = jnp.concatenate([far, key_two, value_two], axis=1)
    mine = in_turn("core", kept, swapped(sent, "core"), 0)
    width = mine.shape[1]
    early, late = mine[:, width - EARLY :], mine[:, : width - EARLY]
    early = lax.all_gather(early, "z", axis=0, tiled=True)
    late_other = swapped(late, "xh")
    rank = lax.axis_index(SEQ).astype(jnp.int32).reshape(1)
    far1 = from_behind(own, 1)
    far2 = from_behind(far, 2)
    far3 = from_behind(far[3 * rows - 512 :], 3)
    grouped = queries.reshape(peers, apart, cols)
    residuals, normed, partials = {}, [], []
    for begin, size, stack in PARTS:
        part = grouped[:, begin : begin + size].reshape(peers * size, cols)
        if partials:
            part, _ = lax.optimization_barrier((part, partials[0]))
        attended = attend(part, far3, far2, far1, own, rank, begin, stack)
        if not partials:
            attended, early, late_other = lax.optimization_barrier((attended, early, late_other))
            late = lax.all_gather(in_turn("xh", late, late_other, 0), "z", axis=0, tiled=True)
            early_other = swapped(early, "xh")
        partials.append(jnp.dot(attended, out_weight, preferred_element_type=jnp.float32).astype(jnp.bfloat16))
    for (begin, size, _), partial in zip(PARTS, partials):
        arrived = over_heads(partial.reshape(peers, size, -1))
        arrived = arrived.astype(jnp.float32).sum(axis=0)
        summed = residual_in[begin : begin + size].astype(jnp.float32) + arrived
        residuals[begin] = summed.astype(jnp.bfloat16)
        own_rows = normalize(summed, norm_gain)
        tiles = jnp.broadcast_to(own_rows[None], (peers, *own_rows.shape))
        normed.append(over_heads(tiles).reshape(peers * size, -1))
    residual_out = jnp.concatenate([residuals[begin] for begin in sorted(residuals)], axis=0)
    early, early_other = (a.reshape(planes, 1, -1, EARLY) for a in (early, early_other))
    early = in_turn("xh", early, early_other, 1).reshape(-1, EARLY)
    ours = jnp.concatenate(normed, axis=0)
    theirs = jnp.concatenate([swapped(block, "core") for block in normed], axis=0)
    both = jnp.concatenate([ours, theirs], axis=0)
    product = jnp.concatenate(
        [jnp.dot(both, w, preferred_element_type=jnp.float32) for w in (late, early)], axis=1
    )
    back = swapped(product[rows:].astype(jnp.bfloat16), "core").astype(jnp.float32)
    gate_sum = jnp.where(gates, product[:rows], back)
    up_sum = jnp.where(gates, back, product[:rows])
    hidden = (jax.nn.silu(gate_sum) * up_sum).astype(jnp.bfloat16)
    pieces, at = {}, 0
    for begin, size, _ in PARTS:
        pieces[begin] = hidden[at : at + peers * size].reshape(peers, size, width)
        at += peers * size
    hidden = jnp.concatenate([pieces[begin] for begin in sorted(pieces)], axis=1).reshape(rows, width)
    return (residual_out, hidden)


def solution(mesh):
    fine = Mesh(np.asarray(mesh.devices).reshape(8, 2, 2, 4, 2), SEQ + HEAD)
    return jax.shard_map(
        body,
        mesh=fine,
        in_specs=(
            P(SEQ, HEAD),
            P(SEQ, None),
            P(SEQ, None),
            P(SEQ, None),
            P(SEQ, None),
            P(SEQ + HEAD, None),
            P(HEAD, None),
            P(),
            P(SEQ, HEAD),
            P(SEQ, HEAD),
        ),
        out_specs=(P(SEQ + HEAD, None), P(SEQ, HEAD)),
        check_vma=False,
    )
```

time: 157 us -> 169 us (1.076)
  the two profiles are of different devices: /device:TPU:100 before, /device:TPU:1 now
where the time goes in v2:
time: 169 us; the launch traced here: 168 us
  starting transfers between devices  51.8 us (31%)
  waiting for transfers between devices  45.2 us (27%)
  Pallas kernels  29.5 us (17%)
  between operations  14.3 us (8%)
  matrix products  14.2 us (8%)
  other arithmetic  7.67 us (5%)
  local copies, waits for them, and re-layouts  5.31 us (3%)
    all_to_all x4, waiting for transfers between devices, over_heads(): return lax.all_to_all(tiles, HEAD, 0, 0, tiled=True)  35.2 us
    pallas_call x2, Pallas kernels, attend(): pl.pallas_call(functools.partial(attention_kernel, heads, begin, stack),...  29.5 us
    ppermute x6, starting transfers between devices, swapped(): return lax.ppermute(block, axis, [(0, 1), (1, 0)])  23.9 us
    all_to_all x4, starting transfers between devices, over_heads(): return lax.all_to_all(tiles, HEAD, 0, 0, tiled=True)  16.5 us
    ppermute x3, starting transfers between devices, from_behind(): return lax.ppermute(block, SEQ, route)  11.4 us
    dot_general x2, matrix products, body(): jnp.dot(both, w, preferred_element_type=jnp.float32)  8.58 us
    all_gather x1, waiting for transfers between devices, body(): early = lax.all_gather(early, 'z', axis=0, tiled=True)  6.03 us
    dot_general x2, matrix products, body(): jnp.dot(attended, out_weight, preferred_element_type=jnp.float32)  5.62 us
  transfers between devices with their start and end apart: 15, of which 8 were waited for; matrix products, arithmetic and copies ran while one was open for 10% of the time, Pallas kernels for 18%

profile of v2, /device:TPU:1, one launch (start us, length us, event | category | flops | bytes accessed | tf_op | source)
XLA Modules:
  0.0 168.1 jit_solution(11527463926599747843)
XLA Ops:
  7.2 1.0 broadcast_select_fusion.6
  8.2 3.3 %collective-permute-start.3 = (bf16[128,896]{1,0:T(8,128)(2,1)S(1)}, bf16[128,896]{1,0:T(8,128)(2,1)S(1)}, u32[]{:S(2)}, u32[]{:S(2)}) collective-permute-start(bf16[128,896]{1,0:T(8,128)(2,1)S(1)} %broadcast_select_fusion.6), channel_id=1, source_target_pairs={{0,8},{8,0},{1,9},{9,1},{2,10},{10,2},{3,11},{11,3},{4,12},{12,4},... | collective-permute-start | bytes 688136 | tf_op jit(solution)/shard_map/ppermute | solution.py:159
  11.5 1.1 collective-permute-done.3
  12.6 1.0 broadcast_select_fusion.5
  15.2 0.8 constant_dynamic-update-slice_fusion.4
  16.0 2.9 %collective-permute-start.1 = (bf16[192,256]{1,0:T(8,128)(2,1)S(1)}, bf16[192,256]{1,0:T(8,128)(2,1)S(1)}, u32[]{:S(2)}, u32[]{:S(2)}) collective-permute-start(bf16[192,256]{1,0:T(8,128)(2,1)S(1)} %get-tuple-element.21), channel_id=1, source_target_pairs={{0,16},{8,24},{16,32},{24,40},{32,48},{40,56},{48,64},{56,72},{64,... | collective-permute-start | bytes 294920 | tf_op jit(solution)/shard_map/ppermute | solution.py:170
  19.0 4.1 %collective-permute-start = (bf16[128,256]{1,0:T(8,128)(2,1)S(1)}, bf16[128,256]{1,0:T(8,128)(2,1)S(1)}, u32[]{:S(2)}, u32[]{:S(2)}) collective-permute-start(bf16[128,256]{1,0:T(8,128)(2,1)S(1)} %slice.48), channel_id=1, source_target_pairs={{0,24},{8,32},{16,40},{24,48},{32,56},{40,64},{48,72},{56,80},{64,... | collective-permute-start | bytes 196616 | tf_op jit(solution)/shard_map/ppermute | solution.py:170
  23.1 0.8 constant_dynamic-update-slice_fusion.3
  23.9 0.8 constant_dynamic-update-slice_fusion.2.own_ref
  24.7 4.3 %collective-permute-start.2 = (bf16[192,512]{1,0:T(8,128)(2,1)S(1)}, bf16[192,512]{1,0:T(8,128)(2,1)S(1)}, u32[]{:S(2)}, u32[]{:S(2)}) collective-permute-start(bf16[192,512]{1,0:T(8,128)(2,1)S(1)} %constant_dynamic-update-slice_fusion.2.own_ref), channel_id=1, source_target_pairs={{0,8},{8,16},{16,24},{24,32},{32,40},{40,48},{48,56},{56,64},{64,7... | collective-permute-start | bytes 589832 | tf_op jit(solution)/shard_map/ppermute | solution.py:170
  29.2 1.7 collective-permute-start.4
  30.8 2.2 %collective-permute-done.2.far1_ref = bf16[192,512]{1,0:T(8,128)(2,1)S(1)} collective-permute-done((bf16[192,512]{1,0:T(8,128)(2,1)S(1)}, bf16[192,512]{1,0:T(8,128)(2,1)S(1)}, u32[]{:S(2)}, u32[]{:S(2)}) %collective-permute-start.2) | collective-permute-done | bytes 196640 | tf_op jit(solution)/shard_map/ppermute | solution.py:170
  33.0 10.5 %attention.2 = bf16[64,512]{1,0:T(8,128)(2,1)S(1)} custom-call(s32[1]{0:T(128)} %bitcast.rank_ref, bf16[64,512]{1,0:T(8,128)(2,1)S(1)} %slice_bitcast_fusion.1.q_ref, bf16[128,256]{1,0:T(8,128)(2,1)S(1)} %collective-permute-done.far3_ref, bf16[192,256]{1,0:T(8,128)(2,1)S(1)} %collective-permute-done.1.far2_ref, ...), custom_call_target="tpu_custom_call" | custom-call | flops 6442450944 | bytes 2000000 | tf_op jit(solution)/shard_map/attention/pallas_call | solution.py:131
  43.6 6.0 %all-gather.3.cloned.1.call-done = bf16[2048,256]{1,0:T(8,128)(2,1)} async-done(((bf16[256,256]{1,0:T(8,128)(2,1)}), bf16[2048,256]{1,0:T(8,128)(2,1)}) %all-gather.3.cloned.1.call-update) | async-done | bytes 1048592 | tf_op jit(solution)/shard_map/all_gather | solution.py:196
  49.7 0.9 pad_maximum_fusion.3
  50.6 3.9 %convolution_convert_fusion.1 = bf16[64,4096]{1,0:T(8,128)(2,1)} fusion(bf16[64,512]{1,0:T(8,128)(2,1)S(1)} %attention.2, bf16[512,4096]{1,0:T(8,128)(2,1)} %param.16), kind=kOutput, calls=%fused_computation.1 | convolution fusion | flops 268697600 | bytes 4784128 | tf_op jit(solution)/shard_map/dot_general | solution.py:213
  54.5 4.2 %all-to-all-start.1 = ((bf16[8,8,4096]{2,1,0:T(8,128)(2,1)}), bf16[8,8,4096]{2,1,0:T(8,128)(2,1)S(1)}, u32[]{:S(2)}, u32[]{:S(2)}) async-start(bf16[8,8,4096]{2,1,0:T(8,128)(2,1)} %bitcast.5), calls=%async_computation.1 | async-start | bytes 1048576 | tf_op jit(solution)/shard_map/all_to_all | solution.py:174
  58.7 19.0 %attention.3 = bf16[128,512]{1,0:T(8,128)(2,1)S(1)} custom-call(s32[1]{0:T(128)} %bitcast.rank_ref, bf16[128,512]{1,0:T(8,128)(2,1)S(1)} %bitcast.22, bf16[128,256]{1,0:T(8,128)(2,1)S(1)} %collective-permute-done.far3_ref, bf16[192,256]{1,0:T(8,128)(2,1)S(1)} %collective-permute-done.1.far2_ref, bf16[192,512]{1,0:T(8,128)(2,1)S(1)} %collective-permute-done.2.far1_ref, ...), custom_call_target="tpu_custom_call" | custom-call | flops 12884901888 | bytes 2000000 | tf_op jit(solution)/shard_map/attention/pallas_call | solution.py:131
  77.7 1.7 %convolution_convert_fusion = bf16[128,4096]{1,0:T(8,128)(2,1)} fusion(bf16[128,512]{1,0:T(8,128)(2,1)S(1)} %attention.3, bf16[512,4096]{1,0:T(8,128)(2,1)S(1)} %copy-done), kind=kOutput, calls=%fused_computation | convolution fusion | flops 537395200 | bytes 5373952 | tf_op jit(solution)/shard_map/dot_general | solution.py:213
  79.5 5.3 %all-to-all-start = ((bf16[8,16,4096]{2,1,0:T(8,128)(2,1)}), bf16[8,16,4096]{2,1,0:T(8,128)(2,1)S(1)}, u32[]{:S(2)}, u32[]{:S(2)}) async-start(bf16[8,16,4096]{2,1,0:T(8,128)(2,1)} %bitcast.4), calls=%async_computation | async-start | bytes 2097152 | tf_op jit(solution)/shard_map/all_to_all | solution.py:174
  84.7 2.8 %collective-permute-start.7 = (bf16[2048,256]{1,0:T(8,128)(2,1)S(1)}, bf16[2048,256]{1,0:T(8,128)(2,1)}, u32[]{:S(2)}, u32[]{:S(2)}) collective-permute-start(bf16[2048,256]{1,0:T(8,128)(2,1)S(1)} %copy-done.1), channel_id=1, source_target_pairs={{0,16},{16,0},{1,17},{17,1},{2,18},{18,2},{3,19},{19,3},{4,20},{20... | collective-permute-start | bytes 3145736 | tf_op jit(solution)/shard_map/ppermute | solution.py:159
  87.7 7.4 %all-to-all-done = bf16[8,16,4096]{2,1,0:T(8,128)(2,1)S(1)} async-done(((bf16[8,16,4096]{2,1,0:T(8,128)(2,1)}), bf16[8,16,4096]{2,1,0:T(8,128)(2,1)S(1)}, u32[]{:S(2)}, u32[]{:S(2)}) %all-to-all-start) | async-done | bytes 1048608 | tf_op jit(solution)/shard_map/all_to_all | solution.py:174
  95.6 1.1 broadcast_in_dim.5
  96.7 3.6 %all-to-all-start.3 = ((bf16[8,16,4096]{2,1,0:T(8,128)(2,1)}), bf16[8,16,4096]{2,1,0:T(8,128)(2,1)S(1)}, u32[]{:S(2)}, u32[]{:S(2)}) async-start(bf16[8,16,4096]{2,1,0:T(8,128)(2,1)} %broadcast_in_dim.5), calls=%async_computation.3 | async-start | bytes 2097152 | tf_op jit(solution)/shard_map/all_to_all | solution.py:174
  100.3 27.6 %all-to-all-done.3 = bf16[8,16,4096]{2,1,0:T(8,128)(2,1)S(1)} async-done(((bf16[8,16,4096]{2,1,0:T(8,128)(2,1)}), bf16[8,16,4096]{2,1,0:T(8,128)(2,1)S(1)}, u32[]{:S(2)}, u32[]{:S(2)}) %all-to-all-start.3) | async-done | bytes 1048608 | tf_op jit(solution)/shard_map/all_to_all | solution.py:174
  127.9 0.9 broadcast_in_dim.4
  128.8 3.5 %all-to-all-start.2 = ((bf16[8,8,4096]{2,1,0:T(8,128)(2,1)}), bf16[8,8,4096]{2,1,0:T(8,128)(2,1)S(1)}, u32[]{:S(2)}, u32[]{:S(2)}) async-start(bf16[8,8,4096]{2,1,0:T(8,128)(2,1)} %broadcast_in_dim.4), calls=%async_computation.2 | async-start | bytes 1048576 | tf_op jit(solution)/shard_map/all_to_all | solution.py:174
  132.3 7.3 %collective-permute-start.6 = (bf16[128,4096]{1,0:T(8,128)(2,1)S(1)}, bf16[128,4096]{1,0:T(8,128)(2,1)}, u32[]{:S(2)}, u32[]{:S(2)}) collective-permute-start(bf16[128,4096]{1,0:T(8,128)(2,1)S(1)} %bitcast.26), channel_id=1, source_target_pairs={{0,8},{8,0},{1,9},{9,1},{2,10},{10,2},{3,11},{11,3},{4,12},{12,4},... | collective-permute-start | bytes 3145736 | tf_op jit(solution)/shard_map/ppermute | solution.py:159
  139.8 8.4 %collective-permute-start.5 = (bf16[64,4096]{1,0:T(8,128)(2,1)S(1)}, bf16[64,4096]{1,0:T(8,128)(2,1)}, u32[]{:S(2)}, u32[]{:S(2)}) collective-permute-start(bf16[64,4096]{1,0:T(8,128)(2,1)S(1)} %bitcast.30), channel_id=1, source_target_pairs={{0,8},{8,0},{1,9},{9,1},{2,10},{10,2},{3,11},{11,3},{4,12},{12,4},... | collective-permute-start | bytes 1572872 | tf_op jit(solution)/shard_map/ppermute | solution.py:159
  148.1 1.4 broadcast_select_fusion.1
  149.8 2.5 %fusion.4 = f32[384,256]{1,0:T(8,128)S(1)} fusion(bf16[4096,256]{1,0:T(8,128)(2,1)S(1)} %bitcast.25, bf16[128,4096]{1,0:T(8,128)(2,1)} %collective-permute-done.6, bf16[64,4096]{1,0:T(8,128)(2,1)} %collective-permute-done.5, bf16[128,4096]{1,0:T(8,128)(2,1)S(1)} %bitcast.27, bf16[64,4096]{1,0:T(8,128)(2,1)S(1)} %bitcast.31), kind=kOutput, calls=%fused_computation.18 | convolution fusion | flops 817889280 | bytes 5636096 | tf_op jit(solution)/shard_map/dot_general | solution.py:229
  152.4 6.1 %fusion.5 = f32[384,640]{1,0:T(8,128)S(1)} fusion(bf16[4096,640]{1,0:T(8,128)(2,1)} %all-gather.5.cloned.1.call-done, bf16[128,4096]{1,0:T(8,128)(2,1)} %collective-permute-done.6, bf16[64,4096]{1,0:T(8,128)(2,1)} %collective-permute-done.5, bf16[128,4096]{1,0:T(8,128)(2,1)S(1)} %bitcast.28, bf16[64,4096]{1,0:T(8,128)(2,1)S(1)} %bitcast.32), kind=kOutput, calls=%fused_computation.19 | convolution fusion | flops 2025848832 | bytes 9371648 | tf_op jit(solution)/shard_map/dot_general | solution.py:229
  (47 shorter events, 5.7 us)
Async XLA Ops:
  7.2 21.9 %copy-start.3 = (bf16[192,512]{1,0:T(8,128)(2,1)S(1)}, bf16[192,512]{1,0:T(8,128)(2,1)}, u32[]{:S(2)}) copy-start(bf16[192,512]{1,0:T(8,128)(2,1)} %param.10) | copy-start | bytes 589828
  7.2 42.4 %all-gather.3.cloned.1.call-start = ((), (), s32[]{:S(2)}) async-start(), calls=%async_computation.4 | async-start | bytes 1179648 | tf_op jit(solution)/shard_map/all_gather | solution.py:196
  8.2 4.4 %collective-permute-start.3 = (bf16[128,896]{1,0:T(8,128)(2,1)S(1)}, bf16[128,896]{1,0:T(8,128)(2,1)S(1)}, u32[]{:S(2)}, u32[]{:S(2)}) collective-permute-start(bf16[128,896]{1,0:T(8,128)(2,1)S(1)} %broadcast_select_fusion.6), channel_id=1, source_target_pairs={{0,8},{8,0},{1,9},{9,1},{2,10},{10,2},{3,11},{11,3},{4,12},{12,4},... | collective-permute-start | bytes 688136 | tf_op jit(solution)/shard_map/ppermute | solution.py:159
  14.3 138.0 %all-gather.5.cloned.1.call-start = ((), (), s32[]{:S(2)}) async-start(), calls=%async_computation.5 | async-start | bytes 5898240 | tf_op jit(solution)/shard_map/all_gather | solution.py:211
  16.0 14.8 %collective-permute-start.1 = (bf16[192,256]{1,0:T(8,128)(2,1)S(1)}, bf16[192,256]{1,0:T(8,128)(2,1)S(1)}, u32[]{:S(2)}, u32[]{:S(2)}) collective-permute-start(bf16[192,256]{1,0:T(8,128)(2,1)S(1)} %get-tuple-element.21), channel_id=1, source_target_pairs={{0,16},{8,24},{16,32},{24,40},{32,48},{40,56},{48,64},{56,72},{64,... | collective-permute-start | bytes 294920 | tf_op jit(solution)/shard_map/ppermute | solution.py:170
  19.0 11.8 %collective-permute-start = (bf16[128,256]{1,0:T(8,128)(2,1)S(1)}, bf16[128,256]{1,0:T(8,128)(2,1)S(1)}, u32[]{:S(2)}, u32[]{:S(2)}) collective-permute-start(bf16[128,256]{1,0:T(8,128)(2,1)S(1)} %slice.48), channel_id=1, source_target_pairs={{0,24},{8,32},{16,40},{24,48},{32,56},{40,64},{48,72},{56,80},{64,... | collective-permute-start | bytes 196616 | tf_op jit(solution)/shard_map/ppermute | solution.py:170
  24.7 8.3 %collective-permute-start.2 = (bf16[192,512]{1,0:T(8,128)(2,1)S(1)}, bf16[192,512]{1,0:T(8,128)(2,1)S(1)}, u32[]{:S(2)}, u32[]{:S(2)}) collective-permute-start(bf16[192,512]{1,0:T(8,128)(2,1)S(1)} %constant_dynamic-update-slice_fusion.2.own_ref), channel_id=1, source_target_pairs={{0,8},{8,16},{16,24},{24,32},{32,40},{40,48},{48,56},{56,64},{64,7... | collective-permute-start | bytes 589832 | tf_op jit(solution)/shard_map/ppermute | solution.py:170
  29.2 14.4 %collective-permute-start.4 = (bf16[256,640]{1,0:T(8,128)(2,1)S(1)}, bf16[256,640]{1,0:T(8,128)(2,1)S(1)}, u32[]{:S(2)}, u32[]{:S(2)}) collective-permute-start(bf16[256,640]{1,0:T(8,128)(2,1)S(1)} %pad_maximum_fusion.7), channel_id=1, source_target_pairs={{0,16},{16,0},{1,17},{17,1},{2,18},{18,2},{3,19},{19,3},{4,20},{20... | collective-permute-start | bytes 983048 | tf_op jit(solution)/shard_map/ppermute | solution.py:159
  54.5 25.0 %all-to-all-start.1 = ((bf16[8,8,4096]{2,1,0:T(8,128)(2,1)}), bf16[8,8,4096]{2,1,0:T(8,128)(2,1)S(1)}, u32[]{:S(2)}, u32[]{:S(2)}) async-start(bf16[8,8,4096]{2,1,0:T(8,128)(2,1)} %bitcast.5), calls=%async_computation.1 | async-start | bytes 1048576 | tf_op jit(solution)/shard_map/all_to_all | solution.py:174
  58.7 19.0 %copy-start = (bf16[512,4096]{1,0:T(8,128)(2,1)S(1)}, bf16[512,4096]{1,0:T(8,128)(2,1)}, u32[]{:S(2)}) copy-start(bf16[512,4096]{1,0:T(8,128)(2,1)} %param.16) | copy-start | bytes 12582916
  77.7 7.0 %copy-start.1 = (bf16[2048,256]{1,0:T(8,128)(2,1)S(1)}, bf16[2048,256]{1,0:T(8,128)(2,1)}, u32[]{:S(2)}) copy-start(bf16[2048,256]{1,0:T(8,128)(2,1)} %all-gather.3.cloned.1.call-done) | copy-start | bytes 3145732
  77.7 9.9 %copy-start.2 = (bf16[24,4096]{1,0:T(8,128)(2,1)S(1)}, bf16[24,4096]{1,0:T(8,128)(2,1)}, u32[]{:S(2)}) copy-start(bf16[24,4096]{1,0:T(8,128)(2,1)} %param.15) | copy-start | bytes 589828
  79.5 16.0 %copy-start.4 = (f32[4096]{0:T(1024)S(1)}, f32[4096]{0:T(1024)}, u32[]{:S(2)}) copy-start(f32[4096]{0:T(1024)} %param.17) | copy-start | bytes 49156
  79.5 15.7 %all-to-all-start = ((bf16[8,16,4096]{2,1,0:T(8,128)(2,1)}), bf16[8,16,4096]{2,1,0:T(8,128)(2,1)S(1)}, u32[]{:S(2)}, u32[]{:S(2)}) async-start(bf16[8,16,4096]{2,1,0:T(8,128)(2,1)} %bitcast.4), calls=%async_computation | async-start | bytes 2097152 | tf_op jit(solution)/shard_map/all_to_all | solution.py:174
  84.7 63.4 %collective-permute-start.7 = (bf16[2048,256]{1,0:T(8,128)(2,1)S(1)}, bf16[2048,256]{1,0:T(8,128)(2,1)}, u32[]{:S(2)}, u32[]{:S(2)}) collective-permute-start(bf16[2048,256]{1,0:T(8,128)(2,1)S(1)} %copy-done.1), channel_id=1, source_target_pairs={{0,16},{16,0},{1,17},{17,1},{2,18},{18,2},{3,19},{19,3},{4,20},{20... | collective-permute-start | bytes 3145736 | tf_op jit(solution)/shard_map/ppermute | solution.py:159
  96.7 31.2 %all-to-all-start.3 = ((bf16[8,16,4096]{2,1,0:T(8,128)(2,1)}), bf16[8,16,4096]{2,1,0:T(8,128)(2,1)S(1)}, u32[]{:S(2)}, u32[]{:S(2)}) async-start(bf16[8,16,4096]{2,1,0:T(8,128)(2,1)} %broadcast_in_dim.5), calls=%async_computation.3 | async-start | bytes 2097152 | tf_op jit(solution)/shard_map/all_to_all | solution.py:174
  128.8 11.0 %all-to-all-start.2 = ((bf16[8,8,4096]{2,1,0:T(8,128)(2,1)}), bf16[8,8,4096]{2,1,0:T(8,128)(2,1)S(1)}, u32[]{:S(2)}, u32[]{:S(2)}) async-start(bf16[8,8,4096]{2,1,0:T(8,128)(2,1)} %broadcast_in_dim.4), calls=%async_computation.2 | async-start | bytes 1048576 | tf_op jit(solution)/shard_map/all_to_all | solution.py:174
  132.3 17.5 %collective-permute-start.6 = (bf16[128,4096]{1,0:T(8,128)(2,1)S(1)}, bf16[128,4096]{1,0:T(8,128)(2,1)}, u32[]{:S(2)}, u32[]{:S(2)}) collective-permute-start(bf16[128,4096]{1,0:T(8,128)(2,1)S(1)} %bitcast.26), channel_id=1, source_target_pairs={{0,8},{8,0},{1,9},{9,1},{2,10},{10,2},{3,11},{11,3},{4,12},{12,4},... | collective-permute-start | bytes 3145736 | tf_op jit(solution)/shard_map/ppermute | solution.py:159
  139.8 10.1 %collective-permute-start.5 = (bf16[64,4096]{1,0:T(8,128)(2,1)S(1)}, bf16[64,4096]{1,0:T(8,128)(2,1)}, u32[]{:S(2)}, u32[]{:S(2)}) collective-permute-start(bf16[64,4096]{1,0:T(8,128)(2,1)S(1)} %bitcast.30), channel_id=1, source_target_pairs={{0,8},{8,0},{1,9},{9,1},{2,10},{10,2},{3,11},{11,3},{4,12},{12,4},... | collective-permute-start | bytes 1572872 | tf_op jit(solution)/shard_map/ppermute | solution.py:159
  158.5 1.7 %collective-permute-start.8 = (bf16[192,896]{1,0:T(8,128)(2,1)S(1)}, bf16[192,896]{1,0:T(8,128)(2,1)S(1)}, u32[]{:S(2)}, u32[]{:S(2)}) collective-permute-start(bf16[192,896]{1,0:T(8,128)(2,1)S(1)} %fusion.3), channel_id=1, source_target_pairs={{0,8},{8,0},{1,9},{9,1},{2,10},{10,2},{3,11},{11,3},{4,12},{12,4},... | collective-permute-start | bytes 1032200 | tf_op jit(solution)/shard_map/ppermute | solution.py:159
Sparse Core Ops, SparseCore 0:
  14.5 35.0 all-gather.2
  51.4 67.1 all-gather.4

commit v3 on v2

--- a/solution.py
+++ b/solution.py
@@ -151,8 +151,79 @@
 
 SEQ = ("z", "xh", "core")
 HEAD = ("y", "xl")
-PARTS = ((16, 8, 2), (0, 16, 1))
-EARLY = 256
+
+
+def prepare_kernel(core_ref, k1_ref, v1_ref, k2_ref, v2_ref, gate_ref, up_ref, own_ref, far_ref, last_ref, kept_ref, sent_ref):
+    width = k1_ref.shape[1]
+    skipped = k1_ref.shape[0] - last_ref.shape[0]
+    for at, ref in enumerate((k1_ref, v1_ref, k2_ref, v2_ref)):
+        own_ref[:, at * width : (at + 1) * width] = ref[...]
+        if at < 2:
+            far_ref[:, at * width : (at + 1) * width] = ref[...]
+            last_ref[:, at * width : (at + 1) * width] = ref[skipped:, :]
+
+    @pl.when(core_ref[0] == 0)
+    def _():
+        kept_ref[...] = gate_ref[...]
+        sent_ref[...] = up_ref[...]
+
+    @pl.when(core_ref[0] != 0)
+    def _():
+        kept_ref[...] = up_ref[...]
+        sent_ref[...] = gate_ref[...]
+
+
+def prepare(core, key_one, value_one, key_two, value_two, gate_weight, up_weight, last):
+    rows, width = key_one.shape
+    shape = lambda *dims: jax.ShapeDtypeStruct(dims, jnp.bfloat16)
+    return pl.pallas_call(
+        prepare_kernel,
+        out_shape=(
+            shape(rows, 4 * width),
+            shape(rows, 2 * width),
+            shape(last, 2 * width),
+            shape(*gate_weight.shape),
+            shape(*gate_weight.shape),
+        ),
+        in_specs=[pl.BlockSpec(memory_space=pltpu.SMEM)] + [pl.BlockSpec()] * 6,
+        out_specs=(pl.BlockSpec(memory_space=pltpu.VMEM),) * 5,
+        compiler_params=pltpu.CompilerParams(vmem_limit_bytes=60 * 2**20),
+        name="prepare",
+    )(core, key_one, value_one, key_two, value_two, gate_weight, up_weight)
+
+
+def product_kernel(x_ref, w_ref, o_ref, total_ref):
+    step = pl.program_id(0)
+    part = jnp.dot(x_ref[...], w_ref[...], preferred_element_type=jnp.float32)
+
+    @pl.when(step == 0)
+    def _():
+        total_ref[...] = part
+
+    @pl.when(step > 0)
+    def _():
+        total_ref[...] += part
+
+    @pl.when(step == pl.num_programs(0) - 1)
+    def _():
+        o_ref[...] = total_ref[...].astype(o_ref.dtype)
+
+
+def product(x, w, dtype):
+    rows, depth = x.shape
+    width, block = w.shape[1], 512
+    return pl.pallas_call(
+        product_kernel,
+        out_shape=jax.ShapeDtypeStruct((rows, width), dtype),
+        grid=(depth // block,),
+        in_specs=[pl.BlockSpec((rows, block), lambda i: (0, i)), pl.BlockSpec((block, width), lambda i: (i, 0))],
+        out_specs=pl.BlockSpec((rows, width), lambda i: (0, 0)),
+        scratch_shapes=[pltpu.VMEM((rows, width), jnp.float32)],
+        compiler_params=pltpu.CompilerParams(vmem_limit_bytes=60 * 2**20),
+        cost_estimate=pl.CostEstimate(
+            flops=2 * rows * depth * width, bytes_accessed=2 * depth * (rows + width), transcendentals=0
+        ),
+    )(x, w)
 
 
 def swapped(block, axis):
@@ -181,62 +252,35 @@
 
 
 def body(queries, key_one, key_two, value_one, value_two, residual_in, out_weight, norm_gain, gate_weight, up_weight):
-    rows, cols = queries.shape
+    rows, _ = queries.shape
     peers = lax.axis_size(HEAD)
-    apart = rows // peers
-    planes = lax.axis_size("z")
-    gates = lax.axis_index("core") == 0
-    kept = jnp.where(gates, gate_weight, up_weight)
-    sent = jnp.where(gates, up_weight, gate_weight)
-    far = jnp.concatenate([key_one, value_one], axis=1)
-    own = jnp.concatenate([far, key_two, value_two], axis=1)
+    core = lax.axis_index("core").astype(jnp.int32)
+    own, far, last, kept, sent = prepare(
+        core.reshape(1), key_one, value_one, key_two, value_two, gate_weight, up_weight, 512 - 2 * rows
+    )
     mine = in_turn("core", kept, swapped(sent, "core"), 0)
-    width = mine.shape[1]
-    early, late = mine[:, width - EARLY :], mine[:, : width - EARLY]
-    early = lax.all_gather(early, "z", axis=0, tiled=True)
-    late_other = swapped(late, "xh")
+    other = swapped(mine, "xh")
     rank = lax.axis_index(SEQ).astype(jnp.int32).reshape(1)
     far1 = from_behind(own, 1)
     far2 = from_behind(far, 2)
-    far3 = from_behind(far[3 * rows - 512 :], 3)
-    grouped = queries.reshape(peers, apart, cols)
-    residuals, normed, partials = {}, [], []
-    for begin, size, stack in PARTS:
-        part = grouped[:, begin : begin + size].reshape(peers * size, cols)
-        if partials:
-            part, _ = lax.optimization_barrier((part, partials[0]))
-        attended = attend(part, far3, far2, far1, own, rank, begin, stack)
-        if not partials:
-            attended, early, late_other = lax.optimization_barrier((attended, early, late_other))
-            late = lax.all_gather(in_turn("xh", late, late_other, 0), "z", axis=0, tiled=True)
-            early_other = swapped(early, "xh")
-        partials.append(jnp.dot(attended, out_weight, preferred_element_type=jnp.float32).astype(jnp.bfloat16))
-    for (begin, size, _), partial in zip(PARTS, partials):
-        arrived = over_heads(partial.reshape(peers, size, -1))
-        arrived = arrived.astype(jnp.float32).sum(axis=0)
-        summed = residual_in[begin : begin + size].astype(jnp.float32) + arrived
-        residuals[begin] = summed.astype(jnp.bfloat16)
-        own_rows = normalize(summed, norm_gain)
-        tiles = jnp.broadcast_to(own_rows[None], (peers, *own_rows.shape))
-        normed.append(over_heads(tiles).reshape(peers * size, -1))
-    residual_out = jnp.concatenate([residuals[begin] for begin in sorted(residuals)], axis=0)
-    early, early_other = (a.reshape(planes, 1, -1, EARLY) for a in (early, early_other))
-    early = in_turn("xh", early, early_other, 1).reshape(-1, EARLY)
-    ours = jnp.concatenate(normed, axis=0)
-    theirs = jnp.concatenate([swapped(block, "core") for block in normed], axis=0)
-    both = jnp.concatenate([ours, theirs], axis=0)
-    product = jnp.concatenate(
-        [jnp.dot(both, w, preferred_element_type=jnp.float32) for w in (late, early)], axis=1
-    )
-    back = swapped(product[rows:].astype(jnp.bfloat16), "core").astype(jnp.float32)
-    gate_sum = jnp.where(gates, product[:rows], back)
-    up_sum = jnp.where(gates, back, product[:rows])
+    far3 = from_behind(last, 3)
+    joined = in_turn("xh", mine, other, 0)
+    weight = lax.all_gather(joined, "z", axis=0, tiled=True)
+    attended = attend(queries, far3, far2, far1, own, rank, 0, 1)
+    partial = jnp.dot(attended, out_weight, preferred_element_type=jnp.float32).astype(jnp.bfloat16)
+    arrived = over_heads(partial.reshape(peers, rows // peers, -1)).astype(jnp.float32).sum(axis=0)
+    summed = residual_in.astype(jnp.float32) + arrived
+    residual_out = summed.astype(jnp.bfloat16)
+    own_rows = normalize(summed, norm_gain)
+    ours = over_heads(jnp.broadcast_to(own_rows[None], (peers, *own_rows.shape))).reshape(rows, -1)
+    theirs = swapped(ours, "core")
+    for_us = product(ours, weight, jnp.float32)
+    for_them = product(theirs, weight, jnp.bfloat16)
+    back = swapped(for_them, "core").astype(jnp.float32)
+    gates = core == 0
+    gate_sum = jnp.where(gates, for_us, back)
+    up_sum = jnp.where(gates, back, for_us)
     hidden = (jax.nn.silu(gate_sum) * up_sum).astype(jnp.bfloat16)
-    pieces, at = {}, 0
-    for begin, size, _ in PARTS:
-        pieces[begin] = hidden[at : at + peers * size].reshape(peers, size, width)
-        at += peers * size
-    hidden = jnp.concatenate([pieces[begin] for begin in sorted(pieces)], axis=1).reshape(rows, width)
     return (residual_out, hidden)
 
 

time: 169 us -> 155 us (0.917)
  the two profiles are of different devices: /device:TPU:1 before, /device:TPU:100 now
where the time goes in v3:
time: 155 us; the launch traced here: 154 us
  blocking collectives  52.1 us (34%)
  Pallas kernels  45.1 us (29%)
  waiting for transfers between devices  21.7 us (14%)
  between operations  14.2 us (9%)
  starting transfers between devices  13 us (8%)
  other arithmetic  5.36 us (3%)
  local copies, waits for them, and re-layouts  1.65 us (1%)
    all_to_all x2, blocking collectives, over_heads(): return lax.all_to_all(tiles, HEAD, 0, 0, tiled=True)  52.1 us
    pallas_call x1, Pallas kernels, attend(): pl.pallas_call(functools.partial(attention_kernel, heads, begin, stack),...  26.3 us
    ppermute x4, waiting for transfers between devices, swapped(): return lax.ppermute(block, axis, [(0, 1), (1, 0)])  18.7 us
    pallas_call x2, Pallas kernels, product(): pl.pallas_call(product_kernel, out_shape=jax.ShapeDtypeStruct((rows, widt...  16.7 us
    ppermute x3, starting transfers between devices, from_behind(): return lax.ppermute(block, SEQ, route)  12.2 us
  transfers between devices with their start and end apart: 8, of which 4 were waited for; matrix products, arithmetic and copies ran while one was open for 1% of the time, Pallas kernels for 23%

profile of v3, /device:TPU:100, one launch (start us, length us, event | category | flops | bytes accessed | tf_op | source)
XLA Modules:
  0.0 154.1 jit_solution(16879048250598343580)
XLA Ops:
  7.2 0.0 all-gather.2.cloned.1.call-start
  7.2 2.1 %prepare.1 = (bf16[192,512]{1,0:T(8,128)(2,1)}, bf16[192,256]{1,0:T(8,128)(2,1)}, bf16[128,256]{1,0:T(8,128)(2,1)}, bf16[128,896]{1,0:T(8,128)(2,1)}, bf16[128,896]{1,0:T(8,128)(2,1)}) custom-call(s32[1]{0:T(128)} %bitcast.1.core_ref, bf16[192,128]{1,0:T(8,128)(2,1)} %k1_ref.1, bf16[192,128]{1,0:T(8,128)(2,1)} %v1_ref.1, bf16[192,128]{1,0:T(8,128)(2,1)} %k2_ref.1, ...), custom_call_target="tpu_custom_call" | custom-call | tf_op jit(solution)/shard_map/prepare/pallas_call | solution.py:179
  9.4 1.7 %collective-permute-done.3 = bf16[128,896]{1,0:T(8,128)(2,1)S(1)} collective-permute-done((bf16[128,896]{1,0:T(8,128)(2,1)}, bf16[128,896]{1,0:T(8,128)(2,1)S(1)}, u32[]{:S(2)}, u32[]{:S(2)}) %collective-permute-start.3) | collective-permute-done | bytes 229408 | tf_op jit(solution)/shard_map/ppermute | solution.py:230
  11.1 1.0 broadcast_select_fusion.3
  12.1 0.6 collective-permute-start.4
  12.7 13.6 %collective-permute-done.4 = bf16[256,896]{1,0:T(8,128)(2,1)S(1)} collective-permute-done((bf16[256,896]{1,0:T(8,128)(2,1)S(1)}, bf16[256,896]{1,0:T(8,128)(2,1)S(1)}, u32[]{:S(2)}, u32[]{:S(2)}) %collective-permute-start.4) | collective-permute-done | bytes 458784 | tf_op jit(solution)/shard_map/ppermute | solution.py:230
  26.2 0.2 broadcast_select_fusion.1
  26.4 0.0 copy-start.1
  26.4 0.0 copy-start
  26.4 1.0 pad_maximum_fusion
  27.5 0.0 all-gather.2.cloned.1.call-update
  27.5 1.9 %collective-permute-start.2 = (bf16[192,512]{1,0:T(8,128)(2,1)S(1)}, bf16[192,512]{1,0:T(8,128)(2,1)S(1)}, u32[]{:S(2)}, u32[]{:S(2)}) collective-permute-start(bf16[192,512]{1,0:T(8,128)(2,1)S(1)} %copy-done.1), channel_id=1, source_target_pairs={{0,8},{8,16},{16,24},{24,32},{32,40},{40,48},{48,56},{56,64},{64,7... | collective-permute-start | bytes 589832 | tf_op jit(solution)/shard_map/ppermute | solution.py:241
  29.4 5.0 %collective-permute-start.1 = (bf16[192,256]{1,0:T(8,128)(2,1)S(1)}, bf16[192,256]{1,0:T(8,128)(2,1)S(1)}, u32[]{:S(2)}, u32[]{:S(2)}) collective-permute-start(bf16[192,256]{1,0:T(8,128)(2,1)S(1)} %copy-done.7), channel_id=1, source_target_pairs={{0,16},{8,24},{16,32},{24,40},{32,48},{40,56},{48,64},{56,72},{64,... | collective-permute-start | bytes 294920 | tf_op jit(solution)/shard_map/ppermute | solution.py:241
  34.4 5.3 %collective-permute-start = (bf16[128,256]{1,0:T(8,128)(2,1)S(1)}, bf16[128,256]{1,0:T(8,128)(2,1)S(1)}, u32[]{:S(2)}, u32[]{:S(2)}) collective-permute-start(bf16[128,256]{1,0:T(8,128)(2,1)S(1)} %copy-done.8), channel_id=1, source_target_pairs={{0,24},{8,32},{16,40},{24,48},{32,56},{40,64},{48,72},{56,80},{64,... | collective-permute-start | bytes 196616 | tf_op jit(solution)/shard_map/ppermute | solution.py:241
  39.8 3.0 %collective-permute-done.far3_ref = bf16[128,256]{1,0:T(8,128)(2,1)S(1)} collective-permute-done((bf16[128,256]{1,0:T(8,128)(2,1)S(1)}, bf16[128,256]{1,0:T(8,128)(2,1)S(1)}, u32[]{:S(2)}, u32[]{:S(2)}) %collective-permute-start) | collective-permute-done | bytes 65568 | tf_op jit(solution)/shard_map/ppermute | solution.py:241
  42.8 0.0 copy-start.3
  42.8 26.3 %attention.1 = bf16[192,512]{1,0:T(8,128)(2,1)S(1)} custom-call(s32[1]{0:T(128)} %bitcast.rank_ref, bf16[192,512]{1,0:T(8,128)(2,1)S(1)} %copy-done, bf16[128,256]{1,0:T(8,128)(2,1)S(1)} %collective-permute-done.far3_ref, bf16[192,256]{1,0:T(8,128)(2,1)S(1)} %collective-permute-done.1.far2_ref, bf16[192,512]{1,0:T(8,128)(2,1)S(1)} %collective-permute-done.2.far1_ref, ...), custom_call_target="tpu_custom_call" | custom-call | flops 19327352832 | bytes 2000000 | tf_op jit(solution)/shard_map/attention/pallas_call | solution.py:131
  69.1 1.0 convolution_convert_fusion
  70.1 0.0 copy-start.5
  70.1 28.2 %all_to_all.10 = bf16[8,24,4096]{2,1,0:T(8,128)(2,1)S(1)} all-to-all(bf16[8,24,4096]{2,1,0:T(8,128)(2,1)S(1)} %bitcast.8), channel_id=1, replica_groups=mesh['z'=8,'xh'=2,'core'=2,'y'=4,'xl'=2] {'y','xl'}, dimensions={0} | all-to-all | bytes 3145728 | tf_op jit(solution)/shard_map/all_to_all | solution.py:245
  98.3 0.2 convert_reduce_fusion
  98.5 0.2 multiply_reduce_fusion
  98.7 0.3 copy-done.6
  99.0 0.7 multiply_convert_fusion
  99.7 0.2 broadcast_in_dim.2
  99.9 23.9 %all_to_all.11 = bf16[8,24,4096]{2,1,0:T(8,128)(2,1)S(1)} all-to-all(bf16[8,24,4096]{2,1,0:T(8,128)(2,1)S(1)} %broadcast_in_dim.2), channel_id=1, replica_groups=mesh['z'=8,'xh'=2,'core'=2,'y'=4,'xl'=2] {'y','xl'}, dimensions={0} | all-to-all | bytes 3145728 | tf_op jit(solution)/shard_map/all_to_all | solution.py:245
  123.8 3.4 %collective-permute-done.5.x_ref = bf16[192,4096]{1,0:T(8,128)(2,1)S(1)} collective-permute-done((bf16[192,4096]{1,0:T(8,128)(2,1)S(1)}, bf16[192,4096]{1,0:T(8,128)(2,1)S(1)}, u32[]{:S(2)}, u32[]{:S(2)}) %collective-permute-start.5) | collective-permute-done | bytes 1572896 | tf_op jit(solution)/shard_map/ppermute | solution.py:230
  127.2 1.1 copy-done.4
  128.3 8.3 %shard_map.114 = bf16[192,896]{1,0:T(8,128)(2,1)} custom-call(bf16[192,4096]{1,0:T(8,128)(2,1)} %copy-done.4, bf16[4096,896]{1,0:T(8,128)(2,1)} %all-gather.2.cloned.1.call-done.w_ref), custom_call_target="tpu_custom_call" | custom-call | flops 1409286144 | bytes 8912896 | tf_op jit(solution)/shard_map/pallas_call | solution.py:215
  136.6 0.1 collective-permute-start.6
  136.8 8.4 %shard_map.113 = f32[192,896]{1,0:T(8,128)} custom-call(bf16[192,4096]{1,0:T(8,128)(2,1)} %bitcast.7, bf16[4096,896]{1,0:T(8,128)(2,1)} %all-gather.2.cloned.1.call-done.w_ref), custom_call_target="tpu_custom_call" | custom-call | flops 1409286144 | bytes 8912896 | tf_op jit(solution)/shard_map/pallas_call | solution.py:215
  145.2 2.1 %fusion.1 = bf16[192,896]{1,0:T(8,128)(2,1)} fusion(f32[192,896]{1,0:T(8,128)} %shard_map.113, bf16[192,896]{1,0:T(8,128)(2,1)S(1)} %collective-permute-done.6, pred[]{:T(512)S(6)} %eq.7), kind=kLoop, calls=%fused_computation.6 | loop fusion | flops 1548288 | bytes 1376257 | tf_op jit(solution)/shard_map/convert_element_type | solution.py:283
  (20 shorter events, 0.1 us)
Async XLA Ops:
  7.2 120.0 %all-gather.2.cloned.1.call-start = ((), (), s32[]{:S(2)}) async-start(), calls=%async_computation.2 | async-start | bytes 8257536 | tf_op jit(solution)/shard_map/all_gather | solution.py:268
  9.4 1.7 %collective-permute-start.3 = (bf16[128,896]{1,0:T(8,128)(2,1)}, bf16[128,896]{1,0:T(8,128)(2,1)S(1)}, u32[]{:S(2)}, u32[]{:S(2)}) collective-permute-start(bf16[128,896]{1,0:T(8,128)(2,1)} %get-tuple-element.11), channel_id=1, source_target_pairs={{0,8},{8,0},{1,9},{9,1},{2,10},{10,2},{3,11},{11,3},{4,12},{12,4},... | collective-permute-start | bytes 688136 | tf_op jit(solution)/shard_map/ppermute | solution.py:230
  12.1 14.2 %collective-permute-start.4 = (bf16[256,896]{1,0:T(8,128)(2,1)S(1)}, bf16[256,896]{1,0:T(8,128)(2,1)S(1)}, u32[]{:S(2)}, u32[]{:S(2)}) collective-permute-start(bf16[256,896]{1,0:T(8,128)(2,1)S(1)} %pad_maximum_fusion.1), channel_id=1, source_target_pairs={{0,16},{16,0},{1,17},{17,1},{2,18},{18,2},{3,19},{19,3},{4,20},{20... | collective-permute-start | bytes 1376264 | tf_op jit(solution)/shard_map/ppermute | solution.py:230
  26.4 1.1 copy-start.1
  26.4 3.0 %copy-start.7 = (bf16[192,256]{1,0:T(8,128)(2,1)S(1)}, bf16[192,256]{1,0:T(8,128)(2,1)}, u32[]{:S(2)}) copy-start(bf16[192,256]{1,0:T(8,128)(2,1)} %get-tuple-element.8) | copy-start | bytes 294916
  26.4 8.0 %copy-start.8 = (bf16[128,256]{1,0:T(8,128)(2,1)S(1)}, bf16[128,256]{1,0:T(8,128)(2,1)}, u32[]{:S(2)}) copy-start(bf16[128,256]{1,0:T(8,128)(2,1)} %get-tuple-element.7) | copy-start | bytes 196612
  26.4 16.3 %copy-start = (bf16[192,512]{1,0:T(8,128)(2,1)S(1)}, bf16[192,512]{1,0:T(8,128)(2,1)}, u32[]{:S(2)}) copy-start(bf16[192,512]{1,0:T(8,128)(2,1)} %q_ref.1) | copy-start | bytes 589828
  27.5 15.3 %collective-permute-start.2 = (bf16[192,512]{1,0:T(8,128)(2,1)S(1)}, bf16[192,512]{1,0:T(8,128)(2,1)S(1)}, u32[]{:S(2)}, u32[]{:S(2)}) collective-permute-start(bf16[192,512]{1,0:T(8,128)(2,1)S(1)} %copy-done.1), channel_id=1, source_target_pairs={{0,8},{8,16},{16,24},{24,32},{32,40},{40,48},{48,56},{56,64},{64,7... | collective-permute-start | bytes 589832 | tf_op jit(solution)/shard_map/ppermute | solution.py:241
  29.4 13.3 %collective-permute-start.1 = (bf16[192,256]{1,0:T(8,128)(2,1)S(1)}, bf16[192,256]{1,0:T(8,128)(2,1)S(1)}, u32[]{:S(2)}, u32[]{:S(2)}) collective-permute-start(bf16[192,256]{1,0:T(8,128)(2,1)S(1)} %copy-done.7), channel_id=1, source_target_pairs={{0,16},{8,24},{16,32},{24,40},{32,48},{40,56},{48,64},{56,72},{64,... | collective-permute-start | bytes 294920 | tf_op jit(solution)/shard_map/ppermute | solution.py:241
  34.4 8.3 %collective-permute-start = (bf16[128,256]{1,0:T(8,128)(2,1)S(1)}, bf16[128,256]{1,0:T(8,128)(2,1)S(1)}, u32[]{:S(2)}, u32[]{:S(2)}) collective-permute-start(bf16[128,256]{1,0:T(8,128)(2,1)S(1)} %copy-done.8), channel_id=1, source_target_pairs={{0,24},{8,32},{16,40},{24,48},{32,56},{40,64},{48,72},{56,80},{64,... | collective-permute-start | bytes 196616 | tf_op jit(solution)/shard_map/ppermute | solution.py:241
  42.8 26.3 %copy-start.3 = (bf16[512,4096]{1,0:T(8,128)(2,1)S(1)}, bf16[512,4096]{1,0:T(8,128)(2,1)}, u32[]{:S(2)}) copy-start(bf16[512,4096]{1,0:T(8,128)(2,1)} %param.16) | copy-start | bytes 12582916
  70.1 28.4 %copy-start.5 = (bf16[24,4096]{1,0:T(8,128)(2,1)S(1)}, bf16[24,4096]{1,0:T(8,128)(2,1)}, u32[]{:S(2)}) copy-start(bf16[24,4096]{1,0:T(8,128)(2,1)} %param.15) | copy-start | bytes 589828
  98.3 0.7 copy-start.6
  123.8 12.9 %copy-start.2 = (bf16[8,24,4096]{2,1,0:T(8,128)(2,1)}, bf16[8,24,4096]{2,1,0:T(8,128)(2,1)S(1)}, u32[]{:S(2)}) copy-start(bf16[8,24,4096]{2,1,0:T(8,128)(2,1)S(1)} %all_to_all.11) | copy-start | bytes 4718596
  123.8 3.4 %collective-permute-start.5 = (bf16[192,4096]{1,0:T(8,128)(2,1)S(1)}, bf16[192,4096]{1,0:T(8,128)(2,1)S(1)}, u32[]{:S(2)}, u32[]{:S(2)}) collective-permute-start(bf16[192,4096]{1,0:T(8,128)(2,1)S(1)} %bitcast.6), channel_id=1, source_target_pairs={{0,8},{8,0},{1,9},{9,1},{2,10},{10,2},{3,11},{11,3},{4,12},{12,4},... | collective-permute-start | bytes 4718600 | tf_op jit(solution)/shard_map/ppermute | solution.py:230
  127.2 1.1 copy-start.4
  136.6 8.6 %collective-permute-start.6 = (bf16[192,896]{1,0:T(8,128)(2,1)}, bf16[192,896]{1,0:T(8,128)(2,1)S(1)}, u32[]{:S(2)}, u32[]{:S(2)}) collective-permute-start(bf16[192,896]{1,0:T(8,128)(2,1)} %shard_map.114), channel_id=1, source_target_pairs={{0,8},{8,0},{1,9},{9,1},{2,10},{10,2},{3,11},{11,3},{4,12},{12,4},... | collective-permute-start | bytes 1032200 | tf_op jit(solution)/shard_map/ppermute | solution.py:230
Sparse Core Ops, SparseCore 0:
  27.6 85.4 all-gather.1
